TPU v7x, 32 devices: a whole 2x2x4 slice. The times are simulated.
32 devices in a mesh: pts: 4 (over y, core), grid: 8 (over z, x).
Axes of the slice: x: 2, y: 2, z: 4, core: 2. Of those that a mesh axis runs over, the one named last changes fastest.
Arguments:
- features: bfloat16 [32, 524288], P(None, ('pts', 'grid')), may hold values from -6 to 6
- w_in: bfloat16 [32, 64], replicated, may hold values from -1 to 1
- w_mid: bfloat16 [64, 64], replicated, may hold values from -0.75 to 0.75
- w_conv: bfloat16 [2, 3, 3, 3, 64, 64], replicated, may hold values from -0.15625 to 0.15625
- point_frac: float32 [3, 524288], P(None, ('pts', 'grid')), may hold values from 0 to 1
- point_base: int32 [3, 524288], P(None, ('pts', 'grid')), may hold values from 0 to 6, as said below
- slot_dest: int32 [2048], P(('pts', 'grid')), may hold values from 0 to 7, as said below
- slot_tile_block: int32 [2048], P(('pts', 'grid')), may hold values from 0 to 63
- slot_count: int32 [2048], P(('pts', 'grid')), may hold values from 1 to 256, as said below
Outputs:
- point_out: bfloat16 [64, 524288], P(None, ('pts', 'grid'))
Inputs may be any that keep to these rules, and one draw needn't show every extreme that they name: `point_base`: the three rows give base cells along the first, second and third dimension; the first two rows lie in 0 .. 2 and the third in 0 .. 6, so all eight corners of a point lie in its block. `slot_dest`: among the 64 slots of one device at most 16 name the same value; on every device one value is named by exactly 16 slots, the same value on all devices of one index along pts. `slot_count`: every device has a slot with exactly 256 live points.
All inputs are finite; a program needn't handle non-finite values.
Results may differ from a plain program's by a relative error of at most 0.0035.
The roundings to bfloat16 on the way count: a program that leaves them out, or rounds other values in their place, can miss the bound.
Values may be sent and summed in bfloat16 or wider, within the bound.
A program may use at most 128 MiB of HBM per device.

v0:
```python
import jax
import jax.numpy as jnp
from jax import lax
from jax.sharding import PartitionSpec as P

GZ = 8
BLOCK_EDGE_CELLS = 4
TX = 32
TY = 32


def extended(value, sides, width):
    for axis, dim in sides:
        size, length = (lax.axis_size(axis), value.shape[dim])
        up = [(i, (i + 1) % size) for i in range(size - 1)]
        down = [(j, i) for i, j in up]
        last = lax.slice_in_dim(value, length - width, length, axis=dim)
        initial = lax.slice_in_dim(value, 0, width, axis=dim)
        before = lax.ppermute(last, axis, up)
        after = lax.ppermute(initial, axis, down)
        value = jnp.concatenate([before, value, after], axis=dim)
    return value


def point_layer(weight, inputs):
    mixed_sum = lax.dot_general(
        weight, inputs, (((0,), (0,)), ((), ())), preferred_element_type=jnp.float32
    )
    return jax.nn.silu(mixed_sum).astype(jnp.bfloat16)


def axis_weights(offset, corner, length):
    positions = jnp.arange(length, dtype=jnp.int32)[:, None, None]
    below_part = jnp.where(positions == corner[None], 1.0 - offset[None], 0.0)
    above_part = jnp.where(positions == corner[None] + 1, offset[None], 0.0)
    return below_part + above_part


def trilinear(offsets, corners, counts, block_edge, grid_depth):
    slot_width = offsets.shape[2]
    live_mask = (jnp.arange(slot_width, dtype=jnp.int32)[None, :] < counts[:, None]).astype(
        jnp.float32
    )
    along_x = axis_weights(offsets[0], corners[0], block_edge)
    along_y = axis_weights(offsets[1], corners[1], block_edge)
    along_z = axis_weights(offsets[2], corners[2], grid_depth)
    corner_weights = (
        along_x[:, None, None] * along_y[None, :, None] * along_z[None, None, :] * live_mask
    )
    return corner_weights.reshape(
        block_edge * block_edge, grid_depth, offsets.shape[1], slot_width
    ).astype(jnp.bfloat16)


def splat(weights, hidden):
    sums = jnp.einsum("czsp,hsp->sczh", weights, hidden, preferred_element_type=jnp.float32)
    return sums.astype(jnp.bfloat16).reshape(sums.shape[0], sums.shape[1], -1)


def interpolate(weights, blocks):
    cells = blocks.reshape(blocks.shape[0], weights.shape[0], weights.shape[1], -1)
    return jnp.einsum("czsp,sczh->hsp", weights, cells, preferred_element_type=jnp.float32).astype(
        jnp.bfloat16
    )


def blocks_to_tile(sums, block_ids):
    nbx_local = TX // BLOCK_EDGE_CELLS
    nby_local = TY // BLOCK_EDGE_CELLS
    picks = (
        jnp.arange(nbx_local * nby_local, dtype=jnp.int32)[:, None] == block_ids[None, :]
    ).astype(jnp.bfloat16)
    every_channel = sums.shape[2]
    summed_blocks = jnp.dot(
        picks, sums.reshape(sums.shape[0], -1), preferred_element_type=jnp.float32
    ).astype(jnp.bfloat16)
    summed_blocks = summed_blocks.reshape(
        nbx_local, nby_local, BLOCK_EDGE_CELLS, BLOCK_EDGE_CELLS, every_channel
    ).transpose(0, 2, 1, 3, 4)
    return summed_blocks.reshape(TX, TY, every_channel)


def read_blocks(grid_tile, block_ids):
    nbx_local = TX // BLOCK_EDGE_CELLS
    nby_local = TY // BLOCK_EDGE_CELLS
    every_channel = grid_tile.shape[2]
    blocks = grid_tile.reshape(
        nbx_local, BLOCK_EDGE_CELLS, nby_local, BLOCK_EDGE_CELLS, every_channel
    ).transpose(0, 2, 1, 3, 4)
    blocks = blocks.reshape(
        nbx_local * nby_local, BLOCK_EDGE_CELLS * BLOCK_EDGE_CELLS * every_channel
    )
    picks = (
        block_ids[:, None] == jnp.arange(nbx_local * nby_local, dtype=jnp.int32)[None, :]
    ).astype(jnp.bfloat16)
    chosen = jnp.dot(picks, blocks, preferred_element_type=jnp.float32).astype(jnp.bfloat16)
    return chosen.reshape(block_ids.shape[0], BLOCK_EDGE_CELLS * BLOCK_EDGE_CELLS, every_channel)


def banded_weights(kernel, grid_depth):
    depth_range = jnp.arange(grid_depth, dtype=jnp.int32)
    shifts = (
        depth_range[None, :, None]
        == depth_range[None, None, :] + jnp.arange(3, dtype=jnp.int32)[:, None, None] - 1
    ).astype(jnp.bfloat16)
    banded = jnp.einsum("kab,xykij->xyaibj", shifts, kernel, preferred_element_type=jnp.float32)
    return banded.astype(jnp.bfloat16).reshape(
        3, 3, grid_depth * kernel.shape[3], grid_depth * kernel.shape[4]
    )


def convolve(grid_tile, banded):
    padded = extended(grid_tile, (("grid", 0), ("pts", 1)), 1)
    total_sum = jnp.zeros(grid_tile.shape, jnp.float32)
    for shift_x in range(3):
        for shift_y in range(3):
            window = padded[shift_x : shift_x + TX, shift_y : shift_y + TY]
            total_sum = total_sum + lax.dot_general(
                window,
                banded[shift_x, shift_y],
                (((2,), (0,)), ((), ())),
                preferred_element_type=jnp.float32,
            )
    return jax.nn.silu(total_sum).astype(jnp.bfloat16)


def per_device(
    features, w_in, w_mid, w_conv, point_frac, point_base, slot_dest, slot_tile_block, slot_count
):
    slot_total = slot_dest.shape[0]
    slot_width = features.shape[1] // slot_total
    owners = lax.axis_size("grid")
    per_owner = max(2, 2 * slot_total // owners)
    queue_length = owners * per_owner
    hidden_one = point_layer(w_in, features)
    hidden_two = point_layer(w_mid, hidden_one)
    channels = hidden_two.shape[0]
    hidden_two = hidden_two.reshape(channels, slot_total, slot_width)
    offsets = point_frac.reshape(3, slot_total, slot_width)
    corners = point_base.reshape(3, slot_total, slot_width)
    slot_order = jnp.arange(slot_total, dtype=jnp.int32)
    same_owner = (slot_dest[:, None] == slot_dest[None, :]) & (
        slot_order[None, :] < slot_order[:, None]
    )
    rank_within = jnp.sum(same_owner.astype(jnp.int32), axis=1)
    send_place = slot_dest * per_owner + rank_within
    send_match = send_place[None, :] == jnp.arange(queue_length, dtype=jnp.int32)[:, None]
    filled = jnp.any(send_match, axis=1)
    source = jnp.sum(jnp.where(send_match, slot_order[None, :], 0), axis=1)
    sent_block = jnp.where(filled, jnp.take(slot_tile_block, source), -1)
    kernels = [banded_weights(w_conv[layer_index], GZ) for layer_index in range(w_conv.shape[0])]
    weights = trilinear(offsets, corners, slot_count, BLOCK_EDGE_CELLS, GZ)
    local_sums = splat(weights, hidden_two)
    outgoing = jnp.where(
        filled[:, None, None], jnp.take(local_sums, source, axis=0), jnp.zeros((), jnp.bfloat16)
    )
    arrived_ids = lax.all_to_all(sent_block, "grid", split_axis=0, concat_axis=0, tiled=True)
    arrived = lax.all_to_all(outgoing, "grid", split_axis=0, concat_axis=0, tiled=True)
    grid_tile = blocks_to_tile(arrived, arrived_ids)
    for banded in kernels:
        grid_tile = convolve(grid_tile, banded)
    values = read_blocks(grid_tile, arrived_ids)
    returned = lax.all_to_all(values, "grid", split_axis=0, concat_axis=0, tiled=True)
    interp = interpolate(weights, jnp.take(returned, send_place, axis=0))
    point_out = (hidden_two.astype(jnp.float32) + interp.astype(jnp.float32)).astype(jnp.bfloat16)
    return point_out.reshape(channels, slot_total * slot_width)


def solution(mesh):
    return jax.shard_map(
        per_device,
        mesh=mesh,
        in_specs=(
            P(None, ("pts", "grid")),
            P(),
            P(),
            P(),
            P(None, ("pts", "grid")),
            P(None, ("pts", "grid")),
            P(("pts", "grid")),
            P(("pts", "grid")),
            P(("pts", "grid")),
        ),
        out_specs=P(None, ("pts", "grid")),
        check_vma=False,
    )
```

profile of v0, /device:TPU:1, one launch (start us, length us, event | category | flops | bytes accessed | tf_op | source)
XLA Modules:
  0.0 205.8 jit_solution(17021286773261752145)
XLA Ops:
  1.9 1.6 gather_fusion
  4.3 6.3 %all-to-all-start = ((s32[8,16,1]{1,2,0:T(1,128)}), s32[8,16,1]{1,2,0:T(1,128)S(1)}, u32[]{:S(2)}, u32[]{:S(2)}) async-start(s32[8,16,1]{1,2,0:T(1,128)} %bitcast.3), calls=%async_computation | async-start | bytes 8192 | tf_op jit(solution)/shard_map/all_to_all | solution.py:157
  10.6 1.7 slice_reduce_fusion.5
  12.4 1.7 slice_reduce_fusion.4
  16.3 2.7 %multiply_convert_fusion.3 = bf16[64,16384]{1,0:T(8,128)(2,1)S(1)} fusion(bf16[64,64]{1,0:T(8,128)(2,1)S(1)} %copy-done.6, bf16[32,64]{1,0:T(8,128)(2,1)S(1)} %copy-done.7, bf16[32,16384]{1,0:T(8,128)(2,1)S(1)} %copy-done), kind=kOutput, calls=%fused_computation.20 | convolution fusion | flops 211812352 | bytes 3158016 | tf_op jit(solution)/shard_map/dot_general | solution.py:26
  21.4 3.3 %fusion.13 = bf16[64,16,8,64]{3,2,1,0:T(8,128)(2,1)S(1)} fusion(bf16[64,64,256,1]{2,1,0,3:T(8,128)(2,1)S(1)} %bitcast.177, f32[64,256]{1,0:T(8,128)S(1)} %fusion.67, f32[8,64,256]{2,0,1:T(8,128)S(1)} %select_add_fusion, f32[16,64,256]{2,0,1:T(8,128)S(1)} %copy-done.3), kind=kOutput, calls=%fused_computation.29 | convolution fusion | flops 275251200 | bytes 4784128 | tf_op jit(solution)/shard_map/czsp,hsp->sczh/dot_general | solution.py:56
  26.6 1.8 select_select_fusion
  28.5 5.4 %all-to-all-start.1 = ((bf16[128,16,512]{2,1,0:T(8,128)(2,1)}), bf16[128,16,512]{2,1,0:T(8,128)(2,1)S(1)}, u32[]{:S(2)}, u32[]{:S(2)}) async-start(bf16[128,16,512]{2,1,0:T(8,128)(2,1)} %select_select_fusion), calls=%async_computation.1 | async-start | bytes 4194304 | tf_op jit(solution)/shard_map/all_to_all | solution.py:158
  35.1 5.4 %convert_bitcast_fusion.1 = bf16[3,3,8,64,8,64]{5,4,3,1,0,2:T(8,128)(2,1)} fusion(bf16[1,3,3,3,64,64]{5,4,3,2,1,0:T(8,128)(2,1)S(1)} %get-tuple-element.24, s32[3,8]{1,0:T(4,128)S(1)} %add_add_fusion), kind=kOutput, calls=%fused_computation.6 | convolution fusion | flops 16515264 | bytes 4939872 | tf_op jit(solution)/shard_map/kab,xykij->xyaibj/dot_general | solution.py:106
  40.5 8.5 %copy.42 = bf16[3,3,8,64,8,64]{5,4,3,2,1,0:T(8,128)(2,1)} copy(bf16[3,3,8,64,8,64]{5,4,3,1,0,2:T(8,128)(2,1)} %convert_bitcast_fusion.1) | data formatting | bytes 9437184 | tf_op jit(solution)/shard_map/convert_element_type | solution.py:107
  49.0 13.2 %reshape.260 = bf16[3,3,512,512]{3,2,1,0:T(8,128)(2,1)} reshape(bf16[3,3,8,64,8,64]{5,4,3,2,1,0:T(8,128)(2,1)} %copy.42) | data formatting | bytes 9437184 | tf_op jit(solution)/shard_map/reshape | solution.py:107
  62.2 5.4 %convert_bitcast_fusion = bf16[3,3,8,64,8,64]{5,4,3,1,0,2:T(8,128)(2,1)} fusion(bf16[1,3,3,3,64,64]{5,4,3,2,1,0:T(8,128)(2,1)S(1)} %get-tuple-element.23, s32[3,8]{1,0:T(4,128)S(1)} %add_add_fusion), kind=kOutput, calls=%fused_computation.5 | convolution fusion | flops 16515264 | bytes 4939872 | tf_op jit(solution)/shard_map/kab,xykij->xyaibj/dot_general | solution.py:106
  67.6 8.5 %copy.44 = bf16[3,3,8,64,8,64]{5,4,3,2,1,0:T(8,128)(2,1)} copy(bf16[3,3,8,64,8,64]{5,4,3,1,0,2:T(8,128)(2,1)} %convert_bitcast_fusion) | data formatting | bytes 9437184 | tf_op jit(solution)/shard_map/convert_element_type | solution.py:107
  76.1 13.2 %reshape.261 = bf16[3,3,512,512]{3,2,1,0:T(8,128)(2,1)} reshape(bf16[3,3,8,64,8,64]{5,4,3,2,1,0:T(8,128)(2,1)} %copy.44) | data formatting | bytes 9437184 | tf_op jit(solution)/shard_map/reshape | solution.py:107
  93.3 3.4 %collective-permute-start = (bf16[1,32,512]{2,1,0:T(8,128)(2,1)S(1)}, bf16[1,32,512]{2,1,0:T(8,128)(2,1)S(1)}, u32[]{:S(2)}, u32[]{:S(2)}) collective-permute-start(bf16[1,32,512]{2,1,0:T(8,128)(2,1)S(1)} %get-tuple-element.21), channel_id=1, source_target_pairs={{0,1},{1,2},{2,3},{3,4},{4,5},{5,6},{6,7},{8,9},{9,10},{10,11},{11... | collective-permute-start | bytes 98312 | tf_op jit(solution)/shard_map/ppermute | solution.py:19
  96.7 1.6 collective-permute-start.1
  98.3 1.7 fusion.66
  100.1 1.5 collective-permute-done.1
  101.7 6.3 %collective-permute-start.2 = (bf16[34,1,512]{2,1,0:T(2,128)(2,1)S(1)}, bf16[34,1,512]{2,1,0:T(2,128)(2,1)S(1)}, u32[]{:S(2)}, u32[]{:S(2)}) collective-permute-start(bf16[34,1,512]{2,1,0:T(2,128)(2,1)S(1)} %get-tuple-element.18), channel_id=1, source_target_pairs={{0,8},{8,16},{16,24},{1,9},{9,17},{17,25},{2,10},{10,18},{18,26},{... | collective-permute-start | bytes 104456 | tf_op jit(solution)/shard_map/ppermute | solution.py:19
  108.0 2.1 %collective-permute-start.3 = (bf16[34,1,512]{2,1,0:T(2,128)(2,1)S(1)}, bf16[34,1,512]{2,1,0:T(2,128)(2,1)S(1)}, u32[]{:S(2)}, u32[]{:S(2)}) collective-permute-start(bf16[34,1,512]{2,1,0:T(2,128)(2,1)S(1)} %get-tuple-element.17), channel_id=1, source_target_pairs={{8,0},{16,8},{24,16},{9,1},{17,9},{25,17},{10,2},{18,10},{26,18},{... | collective-permute-start | bytes 104456 | tf_op jit(solution)/shard_map/ppermute | solution.py:20
  110.2 1.7 fusion.18
  116.3 1.5 multiply_convert_fusion.6
  117.8 4.0 %collective-permute-start.4 = (bf16[1,32,512]{2,1,0:T(8,128)(2,1)S(1)}, bf16[1,32,512]{2,1,0:T(8,128)(2,1)S(1)}, u32[]{:S(2)}, u32[]{:S(2)}) collective-permute-start(bf16[1,32,512]{2,1,0:T(8,128)(2,1)S(1)} %get-tuple-element.19), channel_id=1, source_target_pairs={{0,1},{1,2},{2,3},{3,4},{4,5},{5,6},{6,7},{8,9},{9,10},{10,11},{11... | collective-permute-start | bytes 98312 | tf_op jit(solution)/shard_map/ppermute | solution.py:19
  123.8 2.6 %collective-permute-done.5 = bf16[1,32,512]{2,1,0:T(8,128)(2,1)S(1)} collective-permute-done((bf16[1,32,512]{2,1,0:T(8,128)(2,1)S(1)}, bf16[1,32,512]{2,1,0:T(8,128)(2,1)S(1)}, u32[]{:S(2)}, u32[]{:S(2)}) %collective-permute-start.5) | collective-permute-done | bytes 32800 | tf_op jit(solution)/shard_map/ppermute | solution.py:20
  126.6 5.1 %collective-permute-start.6 = (bf16[34,1,512]{2,1,0:T(2,128)(2,1)S(1)}, bf16[34,1,512]{2,1,0:T(2,128)(2,1)S(1)}, u32[]{:S(2)}, u32[]{:S(2)}) collective-permute-start(bf16[34,1,512]{2,1,0:T(2,128)(2,1)S(1)} %get-tuple-element.16), channel_id=1, source_target_pairs={{0,8},{8,16},{16,24},{1,9},{9,17},{17,25},{2,10},{10,18},{18,26},{... | collective-permute-start | bytes 104456 | tf_op jit(solution)/shard_map/ppermute | solution.py:19
  131.6 2.2 %collective-permute-start.7 = (bf16[34,1,512]{2,1,0:T(2,128)(2,1)S(1)}, bf16[34,1,512]{2,1,0:T(2,128)(2,1)S(1)}, u32[]{:S(2)}, u32[]{:S(2)}) collective-permute-start(bf16[34,1,512]{2,1,0:T(2,128)(2,1)S(1)} %get-tuple-element.15), channel_id=1, source_target_pairs={{8,0},{16,8},{24,16},{9,1},{17,9},{25,17},{10,2},{18,10},{26,18},{... | collective-permute-start | bytes 104456 | tf_op jit(solution)/shard_map/ppermute | solution.py:20
  135.3 2.0 collective-permute-done.7
  141.7 1.5 multiply_convert_fusion.5
  145.6 2.2 %copy.58 = bf16[16,8,16,512]{3,2,1,0:T(8,128)(2,1)} copy(bf16[16,8,16,512]{3,1,2,0:T(8,128)(2,1)S(1)} %bitcast.171) | data formatting | bytes 4194304
  147.8 4.3 %all-to-all-start.2 = ((bf16[128,16,512]{2,1,0:T(8,128)(2,1)}), bf16[128,16,512]{2,1,0:T(8,128)(2,1)S(1)}, u32[]{:S(2)}, u32[]{:S(2)}) async-start(bf16[128,16,512]{2,1,0:T(8,128)(2,1)} %bitcast.88), calls=%async_computation.2 | async-start | bytes 4194304 | tf_op jit(solution)/shard_map/all_to_all | solution.py:163
  152.0 47.2 %all-to-all-done.2 = bf16[128,16,512]{2,1,0:T(8,128)(2,1)S(1)} async-done(((bf16[128,16,512]{2,1,0:T(8,128)(2,1)}), bf16[128,16,512]{2,1,0:T(8,128)(2,1)S(1)}, u32[]{:S(2)}, u32[]{:S(2)}) %all-to-all-start.2) | async-done | bytes 2097184 | tf_op jit(solution)/shard_map/all_to_all | solution.py:163
  201.0 3.3 %fusion.9 = bf16[64,8,8,256]{3,2,1,0:T(8,128)(2,1)S(1)} fusion(bf16[8,64,8,256]{3,2,1,0:T(8,128)(2,1)} %bitcast.176, f32[64,256]{1,0:T(8,128)S(1)} %fusion.67, f32[8,64,256]{2,0,1:T(8,128)} %copy-done.4, f32[16,64,256]{2,0,1:T(8,128)} %mul.71, bf16[64,16,8,64]{3,2,1,0:T(8,128)(2,1)S(1)} %gather.20, pred[64]{0:T(512)(128)(4,1)S(1)} %get-tuple-element.11), kind=kOutput, calls=%fused_computation.22 | convolution fusion | flops 280494080 | bytes 6881344 | tf_op jit(solution)/shard_map/czsp,sczh->hsp/dot_general | solution.py:62
  (105 shorter events, 32.3 us)
Async XLA Ops:
  0.0 16.3 %copy-start = (bf16[32,16384]{1,0:T(8,128)(2,1)S(1)}, bf16[32,16384]{1,0:T(8,128)(2,1)}, u32[]{:S(2)}) copy-start(bf16[32,16384]{1,0:T(8,128)(2,1)} %param.9) | copy-start | bytes 3145732
  4.3 24.2 %all-to-all-start = ((s32[8,16,1]{1,2,0:T(1,128)}), s32[8,16,1]{1,2,0:T(1,128)S(1)}, u32[]{:S(2)}, u32[]{:S(2)}) async-start(s32[8,16,1]{1,2,0:T(1,128)} %bitcast.3), calls=%async_computation | async-start | bytes 8192 | tf_op jit(solution)/shard_map/all_to_all | solution.py:157
  14.5 1.8 copy-start.6
  14.5 1.8 copy-start.7
  19.0 1.3 copy-start.2
  19.0 1.3 copy-start.5
  19.1 2.3 %copy-start.3 = (f32[16,64,256]{2,0,1:T(8,128)S(1)}, f32[16,64,256]{2,0,1:T(8,128)}, u32[]{:S(2)}) copy-start(f32[16,64,256]{2,0,1:T(8,128)} %mul.71) | copy-start | bytes 3145732
  20.6 0.8 copy-start.4
  28.5 62.2 %all-to-all-start.1 = ((bf16[128,16,512]{2,1,0:T(8,128)(2,1)}), bf16[128,16,512]{2,1,0:T(8,128)(2,1)S(1)}, u32[]{:S(2)}, u32[]{:S(2)}) async-start(bf16[128,16,512]{2,1,0:T(8,128)(2,1)} %select_select_fusion), calls=%async_computation.1 | async-start | bytes 4194304 | tf_op jit(solution)/shard_map/all_to_all | solution.py:158
  92.5 19.5 %slice-start.2 = ((s8[4718592]{0:T(1024)(128)(4,1)}), s8[524288]{0:T(1024)(128)(4,1)S(1)}, s32[]{:S(2)}) async-start(s8[4718592]{0:T(1024)(128)(4,1)} %bitcast.168), calls=%async_computation.5 | async-start | bytes 1048576
  93.3 6.7 %collective-permute-start = (bf16[1,32,512]{2,1,0:T(8,128)(2,1)S(1)}, bf16[1,32,512]{2,1,0:T(8,128)(2,1)S(1)}, u32[]{:S(2)}, u32[]{:S(2)}) collective-permute-start(bf16[1,32,512]{2,1,0:T(8,128)(2,1)S(1)} %get-tuple-element.21), channel_id=1, source_target_pairs={{0,1},{1,2},{2,3},{3,4},{4,5},{5,6},{6,7},{8,9},{9,10},{10,11},{11... | collective-permute-start | bytes 98312 | tf_op jit(solution)/shard_map/ppermute | solution.py:19
  96.7 15.2 %slice-start.3 = ((s8[4718592]{0:T(1024)(128)(4,1)}), s8[4194304]{0:T(1024)(128)(4,1)S(1)}, s32[]{:S(2)}) async-start(s8[4718592]{0:T(1024)(128)(4,1)} %bitcast.168), calls=%async_computation.6 | async-start | bytes 8388608
  96.7 4.9 %collective-permute-start.1 = (bf16[1,32,512]{2,1,0:T(8,128)(2,1)S(1)}, bf16[1,32,512]{2,1,0:T(8,128)(2,1)S(1)}, u32[]{:S(2)}, u32[]{:S(2)}) collective-permute-start(bf16[1,32,512]{2,1,0:T(8,128)(2,1)S(1)} %get-tuple-element.22), channel_id=1, source_target_pairs={{1,0},{2,1},{3,2},{4,3},{5,4},{6,5},{7,6},{9,8},{10,9},{11,10},{12... | collective-permute-start | bytes 98312 | tf_op jit(solution)/shard_map/ppermute | solution.py:20
  101.7 10.9 %collective-permute-start.2 = (bf16[34,1,512]{2,1,0:T(2,128)(2,1)S(1)}, bf16[34,1,512]{2,1,0:T(2,128)(2,1)S(1)}, u32[]{:S(2)}, u32[]{:S(2)}) collective-permute-start(bf16[34,1,512]{2,1,0:T(2,128)(2,1)S(1)} %get-tuple-element.18), channel_id=1, source_target_pairs={{0,8},{8,16},{16,24},{1,9},{9,17},{17,25},{2,10},{10,18},{18,26},{... | collective-permute-start | bytes 104456 | tf_op jit(solution)/shard_map/ppermute | solution.py:19
  108.0 6.1 %collective-permute-start.3 = (bf16[34,1,512]{2,1,0:T(2,128)(2,1)S(1)}, bf16[34,1,512]{2,1,0:T(2,128)(2,1)S(1)}, u32[]{:S(2)}, u32[]{:S(2)}) collective-permute-start(bf16[34,1,512]{2,1,0:T(2,128)(2,1)S(1)} %get-tuple-element.17), channel_id=1, source_target_pairs={{8,0},{16,8},{24,16},{9,1},{17,9},{25,17},{10,2},{18,10},{26,18},{... | collective-permute-start | bytes 104456 | tf_op jit(solution)/shard_map/ppermute | solution.py:20
  115.5 7.6 %slice-start = ((s8[4718592]{0:T(1024)(128)(4,1)}), s8[4194304]{0:T(1024)(128)(4,1)S(1)}, s32[]{:S(2)}) async-start(s8[4718592]{0:T(1024)(128)(4,1)} %bitcast.166), calls=%async_computation.3 | async-start | bytes 8388608
  116.3 6.8 %slice-start.1 = ((s8[4718592]{0:T(1024)(128)(4,1)}), s8[524288]{0:T(1024)(128)(4,1)S(1)}, s32[]{:S(2)}) async-start(s8[4718592]{0:T(1024)(128)(4,1)} %bitcast.166), calls=%async_computation.4 | async-start | bytes 1048576
  117.8 6.0 %collective-permute-start.4 = (bf16[1,32,512]{2,1,0:T(8,128)(2,1)S(1)}, bf16[1,32,512]{2,1,0:T(8,128)(2,1)S(1)}, u32[]{:S(2)}, u32[]{:S(2)}) collective-permute-start(bf16[1,32,512]{2,1,0:T(8,128)(2,1)S(1)} %get-tuple-element.19), channel_id=1, source_target_pairs={{0,1},{1,2},{2,3},{3,4},{4,5},{5,6},{6,7},{8,9},{9,10},{10,11},{11... | collective-permute-start | bytes 98312 | tf_op jit(solution)/shard_map/ppermute | solution.py:19
  121.8 4.7 %collective-permute-start.5 = (bf16[1,32,512]{2,1,0:T(8,128)(2,1)S(1)}, bf16[1,32,512]{2,1,0:T(8,128)(2,1)S(1)}, u32[]{:S(2)}, u32[]{:S(2)}) collective-permute-start(bf16[1,32,512]{2,1,0:T(8,128)(2,1)S(1)} %get-tuple-element.20), channel_id=1, source_target_pairs={{1,0},{2,1},{3,2},{4,3},{5,4},{6,5},{7,6},{9,8},{10,9},{11,10},{12... | collective-permute-start | bytes 98312 | tf_op jit(solution)/shard_map/ppermute | solution.py:20
  126.6 8.7 %collective-permute-start.6 = (bf16[34,1,512]{2,1,0:T(2,128)(2,1)S(1)}, bf16[34,1,512]{2,1,0:T(2,128)(2,1)S(1)}, u32[]{:S(2)}, u32[]{:S(2)}) collective-permute-start(bf16[34,1,512]{2,1,0:T(2,128)(2,1)S(1)} %get-tuple-element.16), channel_id=1, source_target_pairs={{0,8},{8,16},{16,24},{1,9},{9,17},{17,25},{2,10},{10,18},{18,26},{... | collective-permute-start | bytes 104456 | tf_op jit(solution)/shard_map/ppermute | solution.py:19
  131.6 5.6 %collective-permute-start.7 = (bf16[34,1,512]{2,1,0:T(2,128)(2,1)S(1)}, bf16[34,1,512]{2,1,0:T(2,128)(2,1)S(1)}, u32[]{:S(2)}, u32[]{:S(2)}) collective-permute-start(bf16[34,1,512]{2,1,0:T(2,128)(2,1)S(1)} %get-tuple-element.15), channel_id=1, source_target_pairs={{8,0},{16,8},{24,16},{9,1},{17,9},{25,17},{10,2},{18,10},{26,18},{... | collective-permute-start | bytes 104456 | tf_op jit(solution)/shard_map/ppermute | solution.py:20
  147.8 51.5 %all-to-all-start.2 = ((bf16[128,16,512]{2,1,0:T(8,128)(2,1)}), bf16[128,16,512]{2,1,0:T(8,128)(2,1)S(1)}, u32[]{:S(2)}, u32[]{:S(2)}) async-start(bf16[128,16,512]{2,1,0:T(8,128)(2,1)} %bitcast.88), calls=%async_computation.2 | async-start | bytes 4194304 | tf_op jit(solution)/shard_map/all_to_all | solution.py:163
  201.0 4.8 %copy-start.1 = (bf16[32,16384]{1,0:T(8,128)(2,1)S(1)}, bf16[32,16384]{1,0:T(8,128)(2,1)}, u32[]{:S(2)}) copy-start(bf16[32,16384]{1,0:T(8,128)(2,1)} %param.9) | copy-start | bytes 3145732
where the time goes:
time: 207 us; the launch traced here: 206 us
  local copies, waits for them, and re-layouts  65.4 us (32%)
  waiting for transfers between devices  53.3 us (26%)
  starting transfers between devices  41.9 us (20%)
  matrix products  37.7 us (18%)
  other arithmetic  6.78 us (3%)
    all_to_all x1, waiting for transfers between devices, per_device(): lax.all_to_all(values, 'grid', split_axis=0, concat_axis=0, tiled=True)  47.2 us
    reshape x2, local copies, waits for them, and re-layouts, banded_weights(): banded.astype(jnp.bfloat16)  26.4 us
    ppermute x4, starting transfers between devices, extended(): before = lax.ppermute(last, axis, up)  18.7 us
    convert_element_type x2, local copies, waits for them, and re-layouts, banded_weights(): banded.astype(jnp.bfloat16)  16.9 us
    dot_general x18, matrix products, convolve(): lax.dot_general(window, banded[shift_x, shift_y], (((2,), (0,)), ((), ())...  16.4 us
    dot_general x2, matrix products, banded_weights(): jnp.einsum('kab,xykij->xyaibj', shifts, kernel, preferred_element_type=jn...  10.8 us
    ppermute x4, starting transfers between devices, extended(): after = lax.ppermute(initial, axis, down)  7.17 us
    all_to_all x1, starting transfers between devices, per_device(): lax.all_to_all(sent_block, 'grid', split_axis=0, concat_axis=0, tiled=True)  6.34 us
  transfers between devices with their start and end apart: 11, of which 4 were waited for; matrix products, arithmetic and copies ran while one was open for 39% of the time, Pallas kernels for 0%

commit v1 on v0

v1 whole, which is shorter than its diff:
```python
import functools

import jax
import jax.numpy as jnp
import numpy as np
from jax import lax
from jax.experimental import pallas as pl
from jax.experimental.pallas import tpu as pltpu
from jax.sharding import PartitionSpec as P

GZ = 8
BLOCK_EDGE_CELLS = 4
TX = 32
TY = 32
ID_LANES = 128
MESH = pl.DeviceIdType.MESH
DIRECTIONS = ((1, 0), (-1, 0), (0, 1), (0, -1), (1, 1), (1, -1), (-1, 1), (-1, -1))


def point_layer(weight, inputs):
    mixed_sum = lax.dot_general(
        weight, inputs, (((0,), (0,)), ((), ())), preferred_element_type=jnp.float32
    )
    return jax.nn.silu(mixed_sum).astype(jnp.bfloat16)


def axis_weights(offset, corner, length):
    positions = jnp.arange(length, dtype=jnp.int32)[:, None, None]
    below_part = jnp.where(positions == corner[None], 1.0 - offset[None], 0.0)
    above_part = jnp.where(positions == corner[None] + 1, offset[None], 0.0)
    return below_part + above_part


def trilinear(offsets, corners, counts, block_edge, grid_depth):
    slot_width = offsets.shape[2]
    live_mask = (jnp.arange(slot_width, dtype=jnp.int32)[None, :] < counts[:, None]).astype(
        jnp.float32
    )
    along_x = axis_weights(offsets[0], corners[0], block_edge)
    along_y = axis_weights(offsets[1], corners[1], block_edge)
    along_z = axis_weights(offsets[2], corners[2], grid_depth)
    corner_weights = (
        along_x[:, None, None] * along_y[None, :, None] * along_z[None, None, :] * live_mask
    )
    return corner_weights.reshape(
        block_edge * block_edge, grid_depth, offsets.shape[1], slot_width
    ).astype(jnp.bfloat16)


def splat(weights, hidden):
    sums = jnp.einsum("czsp,hsp->sczh", weights, hidden, preferred_element_type=jnp.float32)
    return sums.astype(jnp.bfloat16).reshape(sums.shape[0], sums.shape[1], -1)


def interpolate(weights, blocks):
    cells = blocks.reshape(blocks.shape[0], weights.shape[0], weights.shape[1], -1)
    return jnp.einsum("czsp,sczh->hsp", weights, cells, preferred_element_type=jnp.float32).astype(
        jnp.bfloat16
    )


def band_kernel(w_ref, out_ref):
    width = w_ref.shape[2]
    depth = out_ref.shape[1] // width
    out_ref[...] = jnp.zeros_like(out_ref)
    for b in range(depth):
        low, high = max(b - 1, 0), min(b + 2, depth)
        out_ref[0, low * width : high * width, b * width : (b + 1) * width] = w_ref[
            0, (low - b + 1) * width : (high - b + 1) * width, :
        ]


def banded_weights(w_conv, grid_depth):
    layers, channels, outs = w_conv.shape[0], w_conv.shape[4], w_conv.shape[5]
    stacked = w_conv.reshape(layers * 9, 3 * channels, outs)
    return pl.pallas_call(
        band_kernel,
        grid=(layers * 9,),
        in_specs=[pl.BlockSpec((1, 3 * channels, outs), lambda n: (n, 0, 0))],
        out_specs=pl.BlockSpec((1, grid_depth * channels, grid_depth * outs), lambda n: (n, 0, 0)),
        out_shape=jax.ShapeDtypeStruct(
            (layers * 9, grid_depth * channels, grid_depth * outs), jnp.bfloat16
        ),
        cost_estimate=pl.CostEstimate(flops=0, bytes_accessed=20_000_000, transcendentals=0),
    )(stacked)


def halo_selectors():
    edge, nbx, nby = BLOCK_EDGE_CELLS, TX // BLOCK_EDGE_CELLS, TY // BLOCK_EDGE_CELLS
    blocks = nbx * nby
    lane = edge * max(nbx, nby)
    cut_sides = np.zeros((4, lane, edge * blocks), np.float32)
    cut_corners = np.zeros((4, lane, blocks), np.float32)
    for k, (da, db) in enumerate(DIRECTIONS):
        bx, by = (nbx - 1 if da > 0 else 0), (nby - 1 if db > 0 else 0)
        if db == 0:
            for j in range(edge):
                for y in range(nby):
                    cut_sides[k, j * nby + y, j * blocks + bx * nby + y] = 1
        elif da == 0:
            for i in range(edge):
                for x in range(nbx):
                    cut_sides[k, i * nbx + x, i * blocks + x * nby + by] = 1
        else:
            cut_corners[k - 4, :, bx * nby + by] = 1
    put_sides = np.zeros((4, edge, blocks, blocks + lane), np.float32)
    put_corners = np.zeros((4, blocks, blocks + 3 * lane), np.float32)
    for k, (da, db) in enumerate(DIRECTIONS):
        for x in range(nbx):
            for y in range(nby):
                row, sx, sy = x * nby + y, x - da, y - db
                out_x, out_y = not 0 <= sx < nbx, not 0 <= sy < nby
                if da == 0 or db == 0:
                    for phase in range(edge):
                        if out_x:
                            column = blocks + phase * nby + sy
                        elif out_y:
                            column = blocks + phase * nbx + sx
                        else:
                            column = sx * nby + sy
                        put_sides[k, phase, row, column] = 1
                else:
                    i, j = (edge - 1 if da > 0 else 0), (edge - 1 if db > 0 else 0)
                    if out_x and out_y:
                        column = blocks + 2 * lane
                    elif out_x:
                        column = blocks + j * nby + sy
                    elif out_y:
                        column = blocks + lane + i * nbx + sx
                    else:
                        column = sx * nby + sy
                    put_corners[k - 4, row, column] = 1
    return [jnp.asarray(m, jnp.bfloat16) for m in (cut_sides, cut_corners, put_sides, put_corners)]


def select(one_hot, values):
    return jnp.dot(one_hot, values, preferred_element_type=jnp.float32).astype(jnp.bfloat16)


def conv_kernel(
    sizes,
    arrived_ref,
    band_ref,
    cut_sides,
    cut_corners,
    put_sides,
    put_corners,
    out_ref,
    phases,
    around,
    leaving,
    landing,
    send_sem,
    recv_sem,
):
    rows, columns = sizes
    edge, blocks, every = BLOCK_EDGE_CELLS, phases.shape[2], phases.shape[3]
    layers = landing.shape[0]
    me_row, me_column = lax.axis_index("grid"), lax.axis_index("pts")

    def present(da, db):
        row, column = me_row + da, me_column + db
        return (row >= 0) & (row < rows) & (column >= 0) & (column < columns)

    barrier = pltpu.get_barrier_semaphore()
    for da, db in DIRECTIONS:

        @pl.when(present(da, db))
        def _():
            pl.semaphore_signal(
                barrier, inc=1, device_id=(me_column + db, me_row + da), device_id_type=MESH
            )

    queue = arrived_ref.shape[0]
    ids = arrived_ref[:, edge * edge * every :].astype(jnp.float32)[:, :blocks]
    places = lax.broadcasted_iota(jnp.int32, (queue, blocks), 1).astype(jnp.float32)
    picks = jnp.where(ids == places, 1.0, 0.0).astype(jnp.bfloat16)
    for cell in range(edge * edge):
        phases[cell // edge, cell % edge] = lax.dot_general(
            picks,
            arrived_ref[:, cell * every : (cell + 1) * every],
            (((0,), (0,)), ((), ())),
            preferred_element_type=jnp.float32,
        ).astype(jnp.bfloat16)

    tall = 3 - (me_row == 0).astype(jnp.int32) - (me_row == rows - 1).astype(jnp.int32)
    wide = 3 - (me_column == 0).astype(jnp.int32) - (me_column == columns - 1).astype(jnp.int32)
    pl.semaphore_wait(barrier, tall * wide - 1)

    for layer in range(layers):

        def copy(k):
            da, db = DIRECTIONS[k]
            return pltpu.make_async_remote_copy(
                src_ref=leaving.at[layer, k],
                dst_ref=landing.at[layer, k],
                send_sem=send_sem.at[layer, k],
                recv_sem=recv_sem.at[layer, k],
                device_id=(me_column + db, me_row + da),
                device_id_type=MESH,
            )

        for k, (da, db) in enumerate(DIRECTIONS):
            i, j = (edge - 1 if da > 0 else 0), (edge - 1 if db > 0 else 0)
            if db == 0:
                source = phases[i].reshape(edge * blocks, every)
            elif da == 0:
                source = phases[:, j].reshape(edge * blocks, every)
            else:
                source = phases[i, j]
            leaving[layer, k] = select(cut_sides[k] if k < 4 else cut_corners[k - 4], source)

            @pl.when(present(da, db))
            def _():
                copy(k).start()

        around[1 : edge + 1, 1 : edge + 1] = phases[...]
        for k, (da, db) in enumerate(DIRECTIONS):

            @pl.when(present(-da, -db))
            def _():
                copy(k).wait_recv()

            @pl.when(jnp.logical_not(present(-da, -db)))
            def _():
                landing[layer, k] = jnp.zeros(landing.shape[2:], landing.dtype)

        for k, (da, db) in enumerate(DIRECTIONS):
            to_x = 0 if da > 0 else edge + 1
            to_y = 0 if db > 0 else edge + 1
            i, j = (edge - 1 if da > 0 else 0), (edge - 1 if db > 0 else 0)
            if db == 0:
                for phase in range(edge):
                    around[to_x, phase + 1] = select(
                        put_sides[k, phase],
                        jnp.concatenate([phases[i, phase], landing[layer, k]], axis=0),
                    )
            elif da == 0:
                for phase in range(edge):
                    around[phase + 1, to_y] = select(
                        put_sides[k, phase],
                        jnp.concatenate([phases[phase, j], landing[layer, k]], axis=0),
                    )
            else:
                side_x = DIRECTIONS.index((da, 0))
                side_y = DIRECTIONS.index((0, db))
                around[to_x, to_y] = select(
                    put_corners[k - 4],
                    jnp.concatenate(
                        [
                            phases[i, j],
                            landing[layer, side_x],
                            landing[layer, side_y],
                            landing[layer, k],
                        ],
                        axis=0,
                    ),
                )

        def one_row(i, carry):
            total = jnp.zeros((edge * blocks, every), jnp.float32)
            for shift_x in range(3):
                for shift_y in range(3):
                    window = around[i + shift_x, shift_y : shift_y + edge]
                    total = total + jnp.dot(
                        window.reshape(edge * blocks, every),
                        band_ref[layer * 9 + shift_x * 3 + shift_y],
                        preferred_element_type=jnp.float32,
                    )
            activated = total / (1.0 + jnp.exp(-total))
            phases[i] = activated.astype(jnp.bfloat16).reshape(edge, blocks, every)
            return carry

        lax.fori_loop(0, edge, one_row, 0)

    for cell in range(edge * edge):
        out_ref[:, cell * every : (cell + 1) * every] = select(
            picks, phases[cell // edge, cell % edge]
        )
    for layer in range(layers):
        for k, (da, db) in enumerate(DIRECTIONS):

            @pl.when(present(da, db))
            def _():
                pltpu.make_async_remote_copy(
                    src_ref=leaving.at[layer, k],
                    dst_ref=landing.at[layer, k],
                    send_sem=send_sem.at[layer, k],
                    recv_sem=recv_sem.at[layer, k],
                    device_id=(me_column + db, me_row + da),
                    device_id_type=MESH,
                ).wait_send()


def convolve_blocks(arrived, banded, layers):
    edge = BLOCK_EDGE_CELLS
    blocks = (TX // edge) * (TY // edge)
    every = banded.shape[2]
    selectors = halo_selectors()
    halo = (layers, len(DIRECTIONS), selectors[0].shape[1], every)
    return pl.pallas_call(
        functools.partial(conv_kernel, (lax.axis_size("grid"), lax.axis_size("pts"))),
        out_shape=jax.ShapeDtypeStruct((arrived.shape[0], edge * edge * every), jnp.bfloat16),
        in_specs=[pl.BlockSpec(memory_space=pltpu.VMEM)] * 6,
        out_specs=pl.BlockSpec(memory_space=pltpu.VMEM),
        scratch_shapes=[
            pltpu.VMEM((edge, edge, blocks, every), jnp.bfloat16),
            pltpu.VMEM((edge + 2, edge + 2, blocks, every), jnp.bfloat16),
            pltpu.VMEM(halo, jnp.bfloat16),
            pltpu.VMEM(halo, jnp.bfloat16),
            pltpu.SemaphoreType.DMA(halo[:2]),
            pltpu.SemaphoreType.DMA(halo[:2]),
        ],
        compiler_params=pltpu.CompilerParams(collective_id=0, has_side_effects=True),
        cost_estimate=pl.CostEstimate(
            flops=layers * 18 * TX * TY * every * every,
            bytes_accessed=layers * 9 * every * every * 2,
            transcendentals=layers * TX * TY * every,
        ),
    )(arrived, banded, *selectors)


def per_device(
    features, w_in, w_mid, w_conv, point_frac, point_base, slot_dest, slot_tile_block, slot_count
):
    slot_total = slot_dest.shape[0]
    slot_width = features.shape[1] // slot_total
    owners = lax.axis_size("grid")
    per_owner = max(2, 2 * slot_total // owners)
    queue_length = owners * per_owner
    hidden_one = point_layer(w_in, features)
    hidden_two = point_layer(w_mid, hidden_one)
    channels = hidden_two.shape[0]
    hidden_two = hidden_two.reshape(channels, slot_total, slot_width)
    offsets = point_frac.reshape(3, slot_total, slot_width)
    corners = point_base.reshape(3, slot_total, slot_width)
    slot_order = jnp.arange(slot_total, dtype=jnp.int32)
    same_owner = (slot_dest[:, None] == slot_dest[None, :]) & (
        slot_order[None, :] < slot_order[:, None]
    )
    rank_within = jnp.sum(same_owner.astype(jnp.int32), axis=1)
    send_place = slot_dest * per_owner + rank_within
    send_match = send_place[None, :] == jnp.arange(queue_length, dtype=jnp.int32)[:, None]
    sent_block = jnp.sum(jnp.where(send_match, slot_tile_block[None, :] + 1, 0), axis=1) - 1
    send_picks = send_match.astype(jnp.bfloat16)
    banded = banded_weights(w_conv, GZ)
    weights = trilinear(offsets, corners, slot_count, BLOCK_EDGE_CELLS, GZ)
    local_sums = splat(weights, hidden_two).reshape(slot_total, -1)
    outgoing = jnp.dot(send_picks, local_sums, preferred_element_type=jnp.float32)
    outgoing = jnp.concatenate(
        [
            outgoing.astype(jnp.bfloat16),
            jnp.broadcast_to(sent_block[:, None], (queue_length, ID_LANES)).astype(jnp.bfloat16),
        ],
        axis=1,
    )
    arrived = lax.all_to_all(outgoing, "grid", split_axis=0, concat_axis=0, tiled=True)
    values = convolve_blocks(arrived, banded, w_conv.shape[0])
    returned = lax.all_to_all(values, "grid", split_axis=0, concat_axis=0, tiled=True)
    blocks = lax.dot_general(
        send_picks, returned, (((0,), (0,)), ((), ())), preferred_element_type=jnp.float32
    ).astype(jnp.bfloat16)
    interp = interpolate(weights, blocks)
    point_out = (hidden_two.astype(jnp.float32) + interp.astype(jnp.float32)).astype(jnp.bfloat16)
    return point_out.reshape(channels, slot_total * slot_width)


def solution(mesh):
    return jax.shard_map(
        per_device,
        mesh=mesh,
        in_specs=(
            P(None, ("pts", "grid")),
            P(),
            P(),
            P(),
            P(None, ("pts", "grid")),
            P(None, ("pts", "grid")),
            P(("pts", "grid")),
            P(("pts", "grid")),
            P(("pts", "grid")),
        ),
        out_specs=P(None, ("pts", "grid")),
        check_vma=False,
    )
```

time: 207 us -> 175 us (0.85)
  blocking collectives: 0 us -> 51.4 us
  local copies, waits for them, and re-layouts: 65.4 us -> 16.3 us
  Pallas kernels: 0 us -> 44.9 us
  starting transfers between devices: 41.9 us -> 6.34 us
  matrix products: 37.7 us -> 12 us
  waiting for transfers between devices: 53.3 us -> 36.3 us
    all_to_all x0 -> x1, blocking collectives: none -> 51.4 us  [per_device(): lax.all_to_all(values, 'grid', split_axis=0, concat_axis=0, tiled=True)]
    all_to_all x2 -> x0, waiting for transfers between devices: 47.2 us -> none  [the longest x1 47.2 us: per_device(): lax.all_to_all(values, 'grid', split_axis=0, concat_axis=0, tiled=True)]
    pallas_call x0 -> x2, Pallas kernels: none -> 44.9 us  [the longest x1 33.1 us: convolve_blocks(): pl.pallas_call(functools.partial(conv_kernel, (lax.axis_size('grid'), lax...]
    all_to_all x1, waiting for transfers between devices: 0.01 us -> 36.3 us  [per_device(): lax.all_to_all(outgoing, 'grid', split_axis=0, concat_axis=0, tiled=True)]
    dot_general x22 -> x2, matrix products: 28.4 us -> 1.3 us  [the longest x1 0.82 us: per_device(): jnp.dot(send_picks, local_sums, preferred_element_type=jnp.float32)]
    reshape x7 -> x1, local copies, waits for them, and re-layouts: 29.6 us -> 3.32 us  [interpolate(): blocks.reshape(blocks.shape[0], weights.shape[0], weights.shape[1], -1)]
    ppermute x8 -> x0, starting transfers between devices: 25.8 us -> none  [the longest x4 18.7 us: extended(): before = lax.ppermute(last, axis, up)]
    convert_element_type x2 -> x0, local copies, waits for them, and re-layouts: 16.9 us -> none  [banded_weights(): banded.astype(jnp.bfloat16)]
  transfers between devices with their start and end apart: 11 -> 1, of which waited for: 4 -> 1; matrix products, arithmetic and copies ran while one was open for 39% -> 0% of each run, Pallas kernels for 0% -> 7%
where the time goes in v1:
time: 175 us; the launch traced here: 172 us
  blocking collectives  51.4 us (29%)
  Pallas kernels  44.9 us (26%)
  waiting for transfers between devices  36.3 us (21%)
  local copies, waits for them, and re-layouts  16.3 us (9%)
  matrix products  12 us (7%)
  starting transfers between devices  6.34 us (4%)
  other arithmetic  4.75 us (3%)
    all_to_all x1, blocking collectives, per_device(): lax.all_to_all(values, 'grid', split_axis=0, concat_axis=0, tiled=True)  51.4 us
    all_to_all x1, waiting for transfers between devices, per_device(): lax.all_to_all(outgoing, 'grid', split_axis=0, concat_axis=0, tiled=True)  36.3 us
    pallas_call x1, Pallas kernels, convolve_blocks(): pl.pallas_call(functools.partial(conv_kernel, (lax.axis_size('grid'), lax...  33.1 us
    pallas_call x1, Pallas kernels, banded_weights(): pl.pallas_call(band_kernel, grid=(layers * 9,), in_specs=[pl.BlockSpec((1...  11.8 us
    all_to_all x1, starting transfers between devices, per_device(): lax.all_to_all(outgoing, 'grid', split_axis=0, concat_axis=0, tiled=True)  6.34 us
    dot_general x1, matrix products, splat(): jnp.einsum('czsp,hsp->sczh', weights, hidden, preferred_element_type=jnp....  4.29 us
    dot_general x1, matrix products, interpolate(): jnp.einsum('czsp,sczh->hsp', weights, cells, preferred_element_type=jnp.f...  3.77 us
    slice x3, local copies, waits for them, and re-layouts, trilinear(): along_x = axis_weights(offsets[0], corners[0], block_edge)  3.52 us
  transfers between devices with their start and end apart: 1, of which 1 were waited for; matrix products, arithmetic and copies ran while one was open for 0% of the time, Pallas kernels for 7%

profile of v1, /device:TPU:1, one launch (start us, length us, event | category | flops | bytes accessed | tf_op | source)
XLA Modules:
  0.0 172.3 jit_solution(2604886206074358303)
XLA Ops:
  0.0 0.0 copy-start
  0.0 0.9 convert_reduce_fusion
  0.9 0.7 multiply_add_fusion
  1.6 0.1 select_reduce_fusion
  1.7 0.7 fusion.14
  2.5 1.7 slice_reduce_fusion.4
  4.3 1.8 %slice_reduce_fusion.5 = (s32[16384]{0:T(1024)S(1)}, s32[16384]{0:T(1024)S(1)}, s32[16384]{0:T(1024)S(1)}) fusion(s32[3,16384]{1,0:T(4,128)} %param.18), kind=kLoop, calls=%fused_computation.37 | loop fusion | bytes 393216 | tf_op jit(solution)/shard_map/slice | solution.py:39
  6.2 0.3 select_add_fusion.1
  6.5 0.3 broadcast_multiply_fusion
  6.9 1.3 mul.64
  8.2 2.7 %multiply_convert_fusion.3 = bf16[64,16384]{1,0:T(8,128)(2,1)S(1)} fusion(bf16[64,64]{1,0:T(8,128)(2,1)S(1)} %copy-done.6, bf16[32,64]{1,0:T(8,128)(2,1)S(1)} %copy-done.7, bf16[32,16384]{1,0:T(8,128)(2,1)S(1)} %copy-done), kind=kOutput, calls=%fused_computation.15 | convolution fusion | flops 211812352 | bytes 3158016 | tf_op jit(solution)/shard_map/dot_general | solution.py:21
  10.9 0.0 copy-start.2
  10.9 0.5 copy.32
  11.5 0.1 select_add_fusion
  11.6 0.6 copy-done.2
  12.2 0.2 copy-done.5
  12.4 0.5 copy-done.3
  12.9 4.3 %fusion.11 = bf16[64,16,8,64]{3,2,1,0:T(8,128)(2,1)} fusion(bf16[64,64,256,1]{2,1,0,3:T(8,128)(2,1)S(1)} %bitcast.47, f32[64,256]{1,0:T(8,128)S(1)} %fusion.14, f32[8,64,256]{2,0,1:T(8,128)S(1)} %select_add_fusion, f32[16,64,256]{2,0,1:T(8,128)S(1)} %copy-done.3), kind=kOutput, calls=%fused_computation.20 | convolution fusion | flops 275251200 | bytes 4784128 | tf_op jit(solution)/shard_map/czsp,hsp->sczh/dot_general | solution.py:51
  17.2 3.3 %reshape_reshape.3 = bf16[64,8192]{1,0:T(8,128)(2,1)S(1)} reshape(bf16[64,16,8,64]{3,2,1,0:T(8,128)(2,1)} %fusion.11) | data formatting | bytes 2097152 | tf_op jit(solution)/shard_map/reshape;reshape | solution.py:348
  20.5 0.8 convolution_convert_fusion
  21.3 0.1 broadcast_in_dim.92
  21.4 1.5 pad_maximum_fusion
  22.9 6.3 %all-to-all-start = ((bf16[8,16,8320]{2,1,0:T(8,128)(2,1)}), bf16[8,16,8320]{2,1,0:T(8,128)(2,1)S(1)}, u32[]{:S(2)}, u32[]{:S(2)}) async-start(bf16[8,16,8320]{2,1,0:T(8,128)(2,1)} %bitcast.2), calls=%async_computation | async-start | bytes 4259840 | tf_op jit(solution)/shard_map/all_to_all | solution.py:357
  29.3 11.8 %shard_map.127.band_ref = bf16[18,512,512]{2,1,0:T(8,128)(2,1)} custom-call(bf16[18,192,64]{2,1,0:T(8,128)(2,1)} %bitcast.48), custom_call_target="tpu_custom_call" | custom-call | bytes 20000000 | tf_op jit(solution)/shard_map/pallas_call | solution.py:76
  41.1 36.3 %all-to-all-done = bf16[8,16,8320]{2,1,0:T(8,128)(2,1)S(1)} async-done(((bf16[8,16,8320]{2,1,0:T(8,128)(2,1)}), bf16[8,16,8320]{2,1,0:T(8,128)(2,1)S(1)}, u32[]{:S(2)}, u32[]{:S(2)}) %all-to-all-start) | async-done | bytes 2129952 | tf_op jit(solution)/shard_map/all_to_all | solution.py:357
  77.4 1.3 copy-done.1
  78.7 33.1 %shard_map.128 = bf16[128,8192]{1,0:T(8,128)(2,1)} custom-call(bf16[128,8320]{1,0:T(8,128)(2,1)} %bitcast.43, bf16[18,512,512]{2,1,0:T(8,128)(2,1)} %shard_map.127.band_ref, bf16[4,32,256]{2,1,0:T(8,128)(2,1)} %constant.25.clone.cut_sides, bf16[4,32,64]{2,1,0:T(8,128)(2,1)} %constant.26.clone.cut_corners, bf16[4,4,64,96]{3,2,1,0:T(8,128)(2,1)} %constant.27.clone.put_sides, ...), custom_call_target="tpu_custom_call" | custom-call | flops 9663676416 | bytes 9437184 | tf_op jit(solution)/shard_map/pallas_call | solution.py:301
  111.8 51.4 %all_to_all.23 = bf16[8,16,8192]{2,1,0:T(8,128)(2,1)S(1)} all-to-all(bf16[8,16,8192]{2,1,0:T(8,128)(2,1)} %bitcast.46), channel_id=1, replica_groups=mesh['pts'=4,'grid'=8] {'grid'}, dimensions={0} | all-to-all | bytes 4194304 | tf_op jit(solution)/shard_map/all_to_all | solution.py:359
  163.2 0.5 convolution_convert_fusion.1
  163.7 3.3 %reshape.140 = bf16[64,16,8,64]{3,2,1,0:T(8,128)(2,1)} reshape(bf16[64,8192]{1,0:T(8,128)(2,1)S(1)} %convolution_convert_fusion.1) | data formatting | bytes 2097152 | tf_op jit(solution)/shard_map/reshape | solution.py:56
  167.0 3.8 %fusion.9 = bf16[64,8,8,256]{3,2,1,0:T(8,128)(2,1)S(1)} fusion(bf16[8,64,8,256]{3,2,1,0:T(8,128)(2,1)} %bitcast.45, bf16[64,16,8,64]{3,2,1,0:T(8,128)(2,1)} %reshape.140, f32[64,256]{1,0:T(8,128)S(1)} %fusion.14, f32[8,64,256]{2,0,1:T(8,128)} %copy-done.5, f32[16,64,256]{2,0,1:T(8,128)S(1)} %copy-done.4), kind=kOutput, calls=%fused_computation.18 | convolution fusion | flops 279969792 | bytes 6881280 | tf_op jit(solution)/shard_map/czsp,sczh->hsp/dot_general | solution.py:57
  170.8 1.5 copy.31
  (23 shorter events, 0.2 us)
Async XLA Ops:
  0.0 8.2 %copy-start = (bf16[32,16384]{1,0:T(8,128)(2,1)S(1)}, bf16[32,16384]{1,0:T(8,128)(2,1)}, u32[]{:S(2)}) copy-start(bf16[32,16384]{1,0:T(8,128)(2,1)} %param.13) | copy-start | bytes 3145732
  0.0 8.2 %copy-start.6 = (bf16[64,64]{1,0:T(8,128)(2,1)S(1)}, bf16[64,64]{1,0:T(8,128)(2,1)}, u32[]{:S(2)}) copy-start(bf16[64,64]{1,0:T(8,128)(2,1)} %param.15) | copy-start | bytes 24580
  0.0 8.2 %copy-start.7 = (bf16[32,64]{1,0:T(8,128)(2,1)S(1)}, bf16[32,64]{1,0:T(8,128)(2,1)}, u32[]{:S(2)}) copy-start(bf16[32,64]{1,0:T(8,128)(2,1)} %param.14) | copy-start | bytes 12292
  10.9 1.3 copy-start.2
  10.9 2.0 %copy-start.3 = (f32[16,64,256]{2,0,1:T(8,128)S(1)}, f32[16,64,256]{2,0,1:T(8,128)}, u32[]{:S(2)}) copy-start(f32[16,64,256]{2,0,1:T(8,128)} %mul.64) | copy-start | bytes 3145732
  11.6 0.8 copy-start.5
  22.9 54.5 %all-to-all-start = ((bf16[8,16,8320]{2,1,0:T(8,128)(2,1)}), bf16[8,16,8320]{2,1,0:T(8,128)(2,1)S(1)}, u32[]{:S(2)}, u32[]{:S(2)}) async-start(bf16[8,16,8320]{2,1,0:T(8,128)(2,1)} %bitcast.2), calls=%async_computation | async-start | bytes 4259840 | tf_op jit(solution)/shard_map/all_to_all | solution.py:357
  77.4 1.3 copy-start.1
  163.2 3.8 %copy-start.4 = (f32[16,64,256]{2,0,1:T(8,128)S(1)}, f32[16,64,256]{2,0,1:T(8,128)}, u32[]{:S(2)}) copy-start(f32[16,64,256]{2,0,1:T(8,128)} %mul.64) | copy-start | bytes 3145732

commit v2 on v1

--- a/solution.py
+++ b/solution.py
@@ -59,30 +59,20 @@
     )
 
 
-def band_kernel(w_ref, out_ref):
+def build_band(w_ref, band_ref):
     width = w_ref.shape[2]
-    depth = out_ref.shape[1] // width
-    out_ref[...] = jnp.zeros_like(out_ref)
-    for b in range(depth):
-        low, high = max(b - 1, 0), min(b + 2, depth)
-        out_ref[0, low * width : high * width, b * width : (b + 1) * width] = w_ref[
-            0, (low - b + 1) * width : (high - b + 1) * width, :
-        ]
-
-
-def banded_weights(w_conv, grid_depth):
-    layers, channels, outs = w_conv.shape[0], w_conv.shape[4], w_conv.shape[5]
-    stacked = w_conv.reshape(layers * 9, 3 * channels, outs)
-    return pl.pallas_call(
-        band_kernel,
-        grid=(layers * 9,),
-        in_specs=[pl.BlockSpec((1, 3 * channels, outs), lambda n: (n, 0, 0))],
-        out_specs=pl.BlockSpec((1, grid_depth * channels, grid_depth * outs), lambda n: (n, 0, 0)),
-        out_shape=jax.ShapeDtypeStruct(
-            (layers * 9, grid_depth * channels, grid_depth * outs), jnp.bfloat16
-        ),
-        cost_estimate=pl.CostEstimate(flops=0, bytes_accessed=20_000_000, transcendentals=0),
-    )(stacked)
+    depth = band_ref.shape[1] // width
+
+    def one(n, carry):
+        band_ref[n] = jnp.zeros(band_ref.shape[1:], band_ref.dtype)
+        for b in range(depth):
+            low, high = max(b - 1, 0), min(b + 2, depth)
+            band_ref[n, low * width : high * width, b * width : (b + 1) * width] = w_ref[
+                n, (low - b + 1) * width : (high - b + 1) * width, :
+            ]
+        return carry
+
+    lax.fori_loop(0, band_ref.shape[0], one, 0)
 
 
 def halo_selectors():
@@ -139,19 +129,27 @@
 
 def conv_kernel(
     sizes,
-    arrived_ref,
-    band_ref,
+    outgoing_ref,
+    w_ref,
     cut_sides,
     cut_corners,
     put_sides,
     put_corners,
     out_ref,
+    arrived,
+    values,
+    band_ref,
     phases,
     around,
     leaving,
     landing,
     send_sem,
     recv_sem,
+    go_send,
+    go_recv,
+    back_send,
+    back_recv,
+    own_sem,
 ):
     rows, columns = sizes
     edge, blocks, every = BLOCK_EDGE_CELLS, phases.shape[2], phases.shape[3]
@@ -162,30 +160,76 @@
         row, column = me_row + da, me_column + db
         return (row >= 0) & (row < rows) & (column >= 0) & (column < columns)
 
+    def go(t):
+        owner = lax.rem(me_row + t, rows)
+        return pltpu.make_async_remote_copy(
+            src_ref=outgoing_ref.at[owner],
+            dst_ref=arrived.at[me_row],
+            send_sem=go_send.at[t],
+            recv_sem=go_recv.at[t],
+            device_id=(me_column, owner),
+            device_id_type=MESH,
+        )
+
+    def back(i, t):
+        origin = lax.rem(me_row + t, rows)
+        part = pl.ds(i * edge * every, edge * every)
+        return pltpu.make_async_remote_copy(
+            src_ref=values.at[origin, :, part],
+            dst_ref=out_ref.at[me_row, :, part],
+            send_sem=back_send.at[i, t],
+            recv_sem=back_recv.at[i, t],
+            device_id=(me_column, origin),
+            device_id_type=MESH,
+        )
+
+    def back_own(i):
+        part = pl.ds(i * edge * every, edge * every)
+        return pltpu.make_async_copy(
+            values.at[me_row, :, part], out_ref.at[me_row, :, part], own_sem.at[i + 1]
+        )
+
     barrier = pltpu.get_barrier_semaphore()
+    for t in range(1, rows):
+        pl.semaphore_signal(
+            barrier,
+            inc=1,
+            device_id=(me_column, lax.rem(me_row + t, rows)),
+            device_id_type=MESH,
+        )
     for da, db in DIRECTIONS:
-
-        @pl.when(present(da, db))
-        def _():
-            pl.semaphore_signal(
-                barrier, inc=1, device_id=(me_column + db, me_row + da), device_id_type=MESH
-            )
-
-    queue = arrived_ref.shape[0]
-    ids = arrived_ref[:, edge * edge * every :].astype(jnp.float32)[:, :blocks]
+        if db != 0:
+
+            @pl.when(present(da, db))
+            def _():
+                pl.semaphore_signal(
+                    barrier, inc=1, device_id=(me_column + db, me_row + da), device_id_type=MESH
+                )
+
+    tall = 3 - (me_row == 0).astype(jnp.int32) - (me_row == rows - 1).astype(jnp.int32)
+    wide = 2 - (me_column == 0).astype(jnp.int32) - (me_column == columns - 1).astype(jnp.int32)
+    pl.semaphore_wait(barrier, rows - 1 + tall * wide)
+
+    for t in range(1, rows):
+        go(t).start()
+    own = pltpu.make_async_copy(outgoing_ref.at[me_row], arrived.at[me_row], own_sem.at[0])
+    own.start()
+    build_band(w_ref, band_ref)
+    own.wait()
+    for t in range(1, rows):
+        go(t).wait_recv()
+
+    queue = arrived.shape[0] * arrived.shape[1]
+    ids = arrived[:, :, edge * edge * every :].reshape(queue, ID_LANES)
     places = lax.broadcasted_iota(jnp.int32, (queue, blocks), 1).astype(jnp.float32)
-    picks = jnp.where(ids == places, 1.0, 0.0).astype(jnp.bfloat16)
+    picks = jnp.where(ids.astype(jnp.float32)[:, :blocks] == places, 1.0, 0.0).astype(jnp.bfloat16)
     for cell in range(edge * edge):
         phases[cell // edge, cell % edge] = lax.dot_general(
             picks,
-            arrived_ref[:, cell * every : (cell + 1) * every],
+            arrived[:, :, cell * every : (cell + 1) * every].reshape(queue, every),
             (((0,), (0,)), ((), ())),
             preferred_element_type=jnp.float32,
         ).astype(jnp.bfloat16)
-
-    tall = 3 - (me_row == 0).astype(jnp.int32) - (me_row == rows - 1).astype(jnp.int32)
-    wide = 3 - (me_column == 0).astype(jnp.int32) - (me_column == columns - 1).astype(jnp.int32)
-    pl.semaphore_wait(barrier, tall * wide - 1)
 
     for layer in range(layers):
 
@@ -267,16 +311,31 @@
                         band_ref[layer * 9 + shift_x * 3 + shift_y],
                         preferred_element_type=jnp.float32,
                     )
-            activated = total / (1.0 + jnp.exp(-total))
-            phases[i] = activated.astype(jnp.bfloat16).reshape(edge, blocks, every)
+            activated = (total / (1.0 + jnp.exp(-total))).astype(jnp.bfloat16)
+            phases[i] = activated.reshape(edge, blocks, every)
             return carry
 
-        lax.fori_loop(0, edge, one_row, 0)
-
-    for cell in range(edge * edge):
-        out_ref[:, cell * every : (cell + 1) * every] = select(
-            picks, phases[cell // edge, cell % edge]
-        )
+        if layer < layers - 1:
+            lax.fori_loop(0, edge, one_row, 0)
+        else:
+            for i in range(edge):
+                one_row(i, 0)
+                for j in range(edge):
+                    cell = i * edge + j
+                    values[:, :, cell * every : (cell + 1) * every] = select(
+                        picks, phases[i, j]
+                    ).reshape(values.shape[0], values.shape[1], every)
+                for t in range(1, rows):
+                    back(i, t).start()
+                back_own(i).start()
+
+    for t in range(1, rows):
+        go(t).wait_send()
+    for i in range(edge):
+        back_own(i).wait()
+        for t in range(1, rows):
+            back(i, t).wait_recv()
+            back(i, t).wait_send()
     for layer in range(layers):
         for k, (da, db) in enumerate(DIRECTIONS):
 
@@ -292,32 +351,39 @@
                 ).wait_send()
 
 
-def convolve_blocks(arrived, banded, layers):
+def exchange_and_convolve(outgoing, w_conv):
     edge = BLOCK_EDGE_CELLS
     blocks = (TX // edge) * (TY // edge)
-    every = banded.shape[2]
+    layers, channels, outs = w_conv.shape[0], w_conv.shape[4], w_conv.shape[5]
+    every = GZ * channels
+    rows, per_owner = outgoing.shape[:2]
+    stacked = w_conv.reshape(layers * 9, 3 * channels, outs)
     selectors = halo_selectors()
     halo = (layers, len(DIRECTIONS), selectors[0].shape[1], every)
+    queue = (rows, per_owner, edge * edge * every)
     return pl.pallas_call(
         functools.partial(conv_kernel, (lax.axis_size("grid"), lax.axis_size("pts"))),
-        out_shape=jax.ShapeDtypeStruct((arrived.shape[0], edge * edge * every), jnp.bfloat16),
+        out_shape=jax.ShapeDtypeStruct(queue, jnp.bfloat16),
         in_specs=[pl.BlockSpec(memory_space=pltpu.VMEM)] * 6,
         out_specs=pl.BlockSpec(memory_space=pltpu.VMEM),
         scratch_shapes=[
+            pltpu.VMEM(outgoing.shape, jnp.bfloat16),
+            pltpu.VMEM(queue, jnp.bfloat16),
+            pltpu.VMEM((layers * 9, every, every), jnp.bfloat16),
             pltpu.VMEM((edge, edge, blocks, every), jnp.bfloat16),
             pltpu.VMEM((edge + 2, edge + 2, blocks, every), jnp.bfloat16),
             pltpu.VMEM(halo, jnp.bfloat16),
             pltpu.VMEM(halo, jnp.bfloat16),
             pltpu.SemaphoreType.DMA(halo[:2]),
             pltpu.SemaphoreType.DMA(halo[:2]),
+            pltpu.SemaphoreType.DMA((rows,)),
+            pltpu.SemaphoreType.DMA((rows,)),
+            pltpu.SemaphoreType.DMA((edge, rows)),
+            pltpu.SemaphoreType.DMA((edge, rows)),
+            pltpu.SemaphoreType.DMA((edge + 1,)),
         ],
         compiler_params=pltpu.CompilerParams(collective_id=0, has_side_effects=True),
-        cost_estimate=pl.CostEstimate(
-            flops=layers * 18 * TX * TY * every * every,
-            bytes_accessed=layers * 9 * every * every * 2,
-            transcendentals=layers * TX * TY * every,
-        ),
-    )(arrived, banded, *selectors)
+    )(outgoing, stacked, *selectors)
 
 
 def per_device(
@@ -343,7 +409,6 @@
     send_match = send_place[None, :] == jnp.arange(queue_length, dtype=jnp.int32)[:, None]
     sent_block = jnp.sum(jnp.where(send_match, slot_tile_block[None, :] + 1, 0), axis=1) - 1
     send_picks = send_match.astype(jnp.bfloat16)
-    banded = banded_weights(w_conv, GZ)
     weights = trilinear(offsets, corners, slot_count, BLOCK_EDGE_CELLS, GZ)
     local_sums = splat(weights, hidden_two).reshape(slot_total, -1)
     outgoing = jnp.dot(send_picks, local_sums, preferred_element_type=jnp.float32)
@@ -354,9 +419,8 @@
         ],
         axis=1,
     )
-    arrived = lax.all_to_all(outgoing, "grid", split_axis=0, concat_axis=0, tiled=True)
-    values = convolve_blocks(arrived, banded, w_conv.shape[0])
-    returned = lax.all_to_all(values, "grid", split_axis=0, concat_axis=0, tiled=True)
+    returned = exchange_and_convolve(outgoing.reshape(owners, per_owner, -1), w_conv)
+    returned = returned.reshape(queue_length, -1)
     blocks = lax.dot_general(
         send_picks, returned, (((0,), (0,)), ((), ())), preferred_element_type=jnp.float32
     ).astype(jnp.bfloat16)

time: 175 us -> 157 us (0.90)
  the two profiles are of different devices: /device:TPU:1 before, /device:TPU:26 now
where the time goes in v2:
time: 157 us
  Pallas kernels  122 us (78%)
  local copies, waits for them, and re-layouts  15 us (10%)
  matrix products  13.6 us (9%)
  other arithmetic  5.58 us (4%)
    pallas_call x1, Pallas kernels, exchange_and_convolve(): pl.pallas_call(functools.partial(conv_kernel, (lax.axis_size('grid'), lax...  122 us
    dot_general x1, matrix products, splat(): jnp.einsum('czsp,hsp->sczh', weights, hidden, preferred_element_type=jnp....  4.29 us
    dot_general x1, matrix products, interpolate(): jnp.einsum('czsp,sczh->hsp', weights, cells, preferred_element_type=jnp.f...  3.76 us
    reshape x1, local copies, waits for them, and re-layouts, interpolate(): blocks.reshape(blocks.shape[0], weights.shape[0], weights.shape[1], -1)  3.32 us
    slice x3, local copies, waits for them, and re-layouts, trilinear(): along_x = axis_weights(offsets[0], corners[0], block_edge)  3.31 us
    another operation x1, local copies, waits for them, and re-layouts, per_device(): local_sums = splat(weights, hidden_two).reshape(slot_total, -1)  3.31 us

profile of v2, /device:TPU:26, one launch (start us, length us, event | category | flops | bytes accessed | tf_op | source)
XLA Modules:
  0.0 156.9 jit_solution(6897734103220342725)
XLA Ops:
  0.0 0.0 copy-start
  0.0 0.9 convert_reduce_fusion
  0.9 0.7 multiply_add_fusion
  1.6 0.1 select_reduce_fusion
  1.7 0.1 broadcast_in_dim.92
  1.8 0.7 fusion.14
  2.6 1.7 %slice_reduce_fusion.4 = (f32[16384]{0:T(1024)S(1)}, f32[16384]{0:T(1024)S(1)}, f32[16384]{0:T(1024)S(1)}) fusion(f32[3,16384]{1,0:T(4,128)} %param.17), kind=kLoop, calls=%fused_computation.36 | loop fusion | bytes 393216 | tf_op jit(solution)/shard_map/slice | solution.py:39
  4.4 1.6 %slice_reduce_fusion.5 = (s32[16384]{0:T(1024)S(1)}, s32[16384]{0:T(1024)S(1)}, s32[16384]{0:T(1024)S(1)}) fusion(s32[3,16384]{1,0:T(4,128)} %param.18), kind=kLoop, calls=%fused_computation.37 | loop fusion | bytes 393216 | tf_op jit(solution)/shard_map/slice | solution.py:39
  6.1 0.3 select_add_fusion.1
  6.4 0.0 copy-start.5
  6.4 0.0 copy-start.6
  6.4 0.9 select_add_fusion
  7.4 0.3 broadcast_multiply_fusion
  7.7 1.3 mul.64
  9.0 0.0 copy-done
  9.0 0.0 copy-done.5
  9.0 0.0 copy-done.6
  9.0 2.7 %multiply_convert_fusion.3 = bf16[64,16384]{1,0:T(8,128)(2,1)S(1)} fusion(bf16[64,64]{1,0:T(8,128)(2,1)S(1)} %copy-done.5, bf16[32,64]{1,0:T(8,128)(2,1)S(1)} %copy-done.6, bf16[32,16384]{1,0:T(8,128)(2,1)S(1)} %copy-done), kind=kOutput, calls=%fused_computation.15 | convolution fusion | flops 211812352 | bytes 3158016 | tf_op jit(solution)/shard_map/dot_general | solution.py:21
  11.7 0.0 copy-start.1
  11.8 0.5 copy.32
  12.3 0.7 copy-done.1
  13.1 0.7 copy-done.2
  13.7 0.1 copy-done.4
  13.9 4.3 %fusion.11 = bf16[64,16,8,64]{3,2,1,0:T(8,128)(2,1)} fusion(bf16[64,64,256,1]{2,1,0,3:T(8,128)(2,1)S(1)} %bitcast.44, f32[64,256]{1,0:T(8,128)S(1)} %fusion.14, f32[8,64,256]{2,0,1:T(8,128)S(1)} %copy-done.4, f32[16,64,256]{2,0,1:T(8,128)S(1)} %copy-done.2), kind=kOutput, calls=%fused_computation.20 | convolution fusion | flops 275251200 | bytes 4784128 | tf_op jit(solution)/shard_map/czsp,hsp->sczh/dot_general | solution.py:51
  18.2 3.3 %reshape_reshape.3 = bf16[64,8192]{1,0:T(8,128)(2,1)S(1)} reshape(bf16[64,16,8,64]{3,2,1,0:T(8,128)(2,1)} %fusion.11) | data formatting | bytes 2097152 | tf_op jit(solution)/shard_map/reshape;reshape | solution.py:413
  21.5 0.8 convolution_convert_fusion
  22.3 1.5 pad_maximum_fusion
  23.8 122.4 %shard_map.127 = bf16[8,16,8192]{2,1,0:T(8,128)(2,1)} custom-call(bf16[8,16,8320]{2,1,0:T(8,128)(2,1)} %bitcast.40, bf16[18,192,64]{2,1,0:T(8,128)(2,1)} %bitcast.45, bf16[4,32,256]{2,1,0:T(8,128)(2,1)} %constant.25.clone.cut_sides, bf16[4,32,64]{2,1,0:T(8,128)(2,1)} %constant.26.clone.cut_corners, bf16[4,4,64,96]{3,2,1,0:T(8,128)(2,1)} %constant.27.clone.put_sides, ...), custom_call_target="tpu_custom_call" | custom-call | tf_op jit(solution)/shard_map/pallas_call | solution.py:364
  146.2 2.1 %convolution_convert_fusion.1 = bf16[64,8192]{1,0:T(8,128)(2,1)S(1)} fusion(bf16[128,8192]{1,0:T(8,128)(2,1)} %bitcast.41, s32[64]{0:T(128)S(1)} %get-tuple-element.11), kind=kOutput, calls=%fused_computation.2 | convolution fusion | flops 134750208 | bytes 3145984 | tf_op jit(solution)/shard_map/dot_general | solution.py:424
  148.3 3.3 %reshape.144 = bf16[64,16,8,64]{3,2,1,0:T(8,128)(2,1)} reshape(bf16[64,8192]{1,0:T(8,128)(2,1)S(1)} %convolution_convert_fusion.1) | data formatting | bytes 2097152 | tf_op jit(solution)/shard_map/reshape | solution.py:56
  151.6 3.8 %fusion.9 = bf16[64,8,8,256]{3,2,1,0:T(8,128)(2,1)S(1)} fusion(bf16[8,64,8,256]{3,2,1,0:T(8,128)(2,1)} %bitcast.43, bf16[64,16,8,64]{3,2,1,0:T(8,128)(2,1)} %reshape.144, f32[64,256]{1,0:T(8,128)S(1)} %fusion.14, f32[8,64,256]{2,0,1:T(8,128)} %select_add_fusion, f32[16,64,256]{2,0,1:T(8,128)S(1)} %copy-done.3), kind=kOutput, calls=%fused_computation.18 | convolution fusion | flops 279969792 | bytes 6881280 | tf_op jit(solution)/shard_map/czsp,sczh->hsp/dot_general | solution.py:57
  155.4 1.5 copy.31
  (17 shorter events, 0.2 us)
Async XLA Ops:
  0.0 9.0 %copy-start = (bf16[32,16384]{1,0:T(8,128)(2,1)S(1)}, bf16[32,16384]{1,0:T(8,128)(2,1)}, u32[]{:S(2)}) copy-start(bf16[32,16384]{1,0:T(8,128)(2,1)} %param.13) | copy-start | bytes 3145732
  6.4 2.6 %copy-start.5 = (bf16[64,64]{1,0:T(8,128)(2,1)S(1)}, bf16[64,64]{1,0:T(8,128)(2,1)}, u32[]{:S(2)}) copy-start(bf16[64,64]{1,0:T(8,128)(2,1)} %param.15) | copy-start | bytes 24580
  6.4 2.6 %copy-start.6 = (bf16[32,64]{1,0:T(8,128)(2,1)S(1)}, bf16[32,64]{1,0:T(8,128)(2,1)}, u32[]{:S(2)}) copy-start(bf16[32,64]{1,0:T(8,128)(2,1)} %param.14) | copy-start | bytes 12292
  11.7 1.3 copy-start.1
  11.7 2.0 %copy-start.2 = (f32[16,64,256]{2,0,1:T(8,128)S(1)}, f32[16,64,256]{2,0,1:T(8,128)}, u32[]{:S(2)}) copy-start(f32[16,64,256]{2,0,1:T(8,128)} %mul.64) | copy-start | bytes 3145732
  11.8 2.1 %copy-start.4 = (f32[8,64,256]{2,0,1:T(8,128)S(1)}, f32[8,64,256]{2,0,1:T(8,128)}, u32[]{:S(2)}) copy-start(f32[8,64,256]{2,0,1:T(8,128)} %select_add_fusion) | copy-start | bytes 1572868
  148.3 3.3 %copy-start.3 = (f32[16,64,256]{2,0,1:T(8,128)S(1)}, f32[16,64,256]{2,0,1:T(8,128)}, u32[]{:S(2)}) copy-start(f32[16,64,256]{2,0,1:T(8,128)} %mul.64) | copy-start | bytes 3145732

commit v3 on v2

--- a/solution.py
+++ b/solution.py
@@ -129,6 +129,7 @@
 
 def conv_kernel(
     sizes,
+    ids_ref,
     outgoing_ref,
     w_ref,
     cut_sides,
@@ -136,8 +137,10 @@
     put_sides,
     put_corners,
     out_ref,
+    ids,
     arrived,
     values,
+    totals,
     band_ref,
     phases,
     around,
@@ -145,6 +148,8 @@
     landing,
     send_sem,
     recv_sem,
+    id_send,
+    id_recv,
     go_send,
     go_recv,
     back_send,
@@ -160,13 +165,25 @@
         row, column = me_row + da, me_column + db
         return (row >= 0) & (row < rows) & (column >= 0) & (column < columns)
 
-    def go(t):
+    def tell(t):
         owner = lax.rem(me_row + t, rows)
         return pltpu.make_async_remote_copy(
-            src_ref=outgoing_ref.at[owner],
-            dst_ref=arrived.at[me_row],
-            send_sem=go_send.at[t],
-            recv_sem=go_recv.at[t],
+            src_ref=ids_ref.at[owner],
+            dst_ref=ids.at[me_row],
+            send_sem=id_send.at[t],
+            recv_sem=id_recv.at[t],
+            device_id=(me_column, owner),
+            device_id_type=MESH,
+        )
+
+    def go(i, t):
+        owner = lax.rem(me_row + t, rows)
+        part = pl.ds(i * edge * every, edge * every)
+        return pltpu.make_async_remote_copy(
+            src_ref=outgoing_ref.at[owner, :, part],
+            dst_ref=arrived.at[me_row, :, part],
+            send_sem=go_send.at[i, t],
+            recv_sem=go_recv.at[i, t],
             device_id=(me_column, owner),
             device_id_type=MESH,
         )
@@ -211,25 +228,51 @@
     pl.semaphore_wait(barrier, rows - 1 + tall * wide)
 
     for t in range(1, rows):
-        go(t).start()
+        tell(t).start()
+    for i in range(edge):
+        for t in range(1, rows):
+            go(i, t).start()
     own = pltpu.make_async_copy(outgoing_ref.at[me_row], arrived.at[me_row], own_sem.at[0])
     own.start()
+    ids[me_row] = ids_ref[me_row]
     build_band(w_ref, band_ref)
+
+    def inner_terms(layer, source):
+        window = around[source + 1, 1 : edge + 1].reshape(edge * blocks, every)
+        for shift_x in range(3):
+            i = source + 1 - shift_x
+            if 0 <= i < edge:
+                term = jnp.dot(
+                    window,
+                    band_ref[layer * 9 + shift_x * 3 + 1],
+                    preferred_element_type=jnp.float32,
+                )
+                if source == max(i - 1, 0):
+                    totals[i] = term
+                else:
+                    totals[i] += term
+
     own.wait()
     for t in range(1, rows):
-        go(t).wait_recv()
-
+        tell(t).wait_recv()
     queue = arrived.shape[0] * arrived.shape[1]
-    ids = arrived[:, :, edge * edge * every :].reshape(queue, ID_LANES)
+    named = ids[...].reshape(queue, ID_LANES).astype(jnp.float32)[:, :blocks]
     places = lax.broadcasted_iota(jnp.int32, (queue, blocks), 1).astype(jnp.float32)
-    picks = jnp.where(ids.astype(jnp.float32)[:, :blocks] == places, 1.0, 0.0).astype(jnp.bfloat16)
-    for cell in range(edge * edge):
-        phases[cell // edge, cell % edge] = lax.dot_general(
-            picks,
-            arrived[:, :, cell * every : (cell + 1) * every].reshape(queue, every),
-            (((0,), (0,)), ((), ())),
-            preferred_element_type=jnp.float32,
-        ).astype(jnp.bfloat16)
+    picks = jnp.where(named == places, 1.0, 0.0).astype(jnp.bfloat16)
+    for i in range(edge):
+        for t in range(1, rows):
+            go(i, t).wait_recv()
+        for j in range(edge):
+            cell = i * edge + j
+            phases[i, j] = lax.dot_general(
+                picks,
+                arrived[:, :, cell * every : (cell + 1) * every].reshape(queue, every),
+                (((0,), (0,)), ((), ())),
+                preferred_element_type=jnp.float32,
+            ).astype(jnp.bfloat16)
+        around[i + 1, 1 : edge + 1] = phases[i]
+        if i < edge - 1:
+            inner_terms(0, i)
 
     for layer in range(layers):
 
@@ -258,7 +301,12 @@
             def _():
                 copy(k).start()
 
-        around[1 : edge + 1, 1 : edge + 1] = phases[...]
+        if layer == 0:
+            inner_terms(0, edge - 1)
+        else:
+            for i in range(edge):
+                around[i + 1, 1 : edge + 1] = phases[i]
+                inner_terms(layer, i)
         for k, (da, db) in enumerate(DIRECTIONS):
 
             @pl.when(present(-da, -db))
@@ -301,10 +349,12 @@
                     ),
                 )
 
-        def one_row(i, carry):
-            total = jnp.zeros((edge * blocks, every), jnp.float32)
+        for i in range(edge):
+            total = totals[i]
             for shift_x in range(3):
                 for shift_y in range(3):
+                    if shift_y == 1 and 1 <= i + shift_x <= edge:
+                        continue
                     window = around[i + shift_x, shift_y : shift_y + edge]
                     total = total + jnp.dot(
                         window.reshape(edge * blocks, every),
@@ -313,13 +363,7 @@
                     )
             activated = (total / (1.0 + jnp.exp(-total))).astype(jnp.bfloat16)
             phases[i] = activated.reshape(edge, blocks, every)
-            return carry
-
-        if layer < layers - 1:
-            lax.fori_loop(0, edge, one_row, 0)
-        else:
-            for i in range(edge):
-                one_row(i, 0)
+            if layer == layers - 1:
                 for j in range(edge):
                     cell = i * edge + j
                     values[:, :, cell * every : (cell + 1) * every] = select(
@@ -330,7 +374,9 @@
                 back_own(i).start()
 
     for t in range(1, rows):
-        go(t).wait_send()
+        tell(t).wait_send()
+        for i in range(edge):
+            go(i, t).wait_send()
     for i in range(edge):
         back_own(i).wait()
         for t in range(1, rows):
@@ -351,7 +397,7 @@
                 ).wait_send()
 
 
-def exchange_and_convolve(outgoing, w_conv):
+def exchange_and_convolve(sent_ids, outgoing, w_conv):
     edge = BLOCK_EDGE_CELLS
     blocks = (TX // edge) * (TY // edge)
     layers, channels, outs = w_conv.shape[0], w_conv.shape[4], w_conv.shape[5]
@@ -364,11 +410,13 @@
     return pl.pallas_call(
         functools.partial(conv_kernel, (lax.axis_size("grid"), lax.axis_size("pts"))),
         out_shape=jax.ShapeDtypeStruct(queue, jnp.bfloat16),
-        in_specs=[pl.BlockSpec(memory_space=pltpu.VMEM)] * 6,
+        in_specs=[pl.BlockSpec(memory_space=pltpu.VMEM)] * 7,
         out_specs=pl.BlockSpec(memory_space=pltpu.VMEM),
         scratch_shapes=[
-            pltpu.VMEM(outgoing.shape, jnp.bfloat16),
+            pltpu.VMEM(sent_ids.shape, jnp.bfloat16),
             pltpu.VMEM(queue, jnp.bfloat16),
+            pltpu.VMEM(queue, jnp.bfloat16),
+            pltpu.VMEM((edge, edge * blocks, every), jnp.float32),
             pltpu.VMEM((layers * 9, every, every), jnp.bfloat16),
             pltpu.VMEM((edge, edge, blocks, every), jnp.bfloat16),
             pltpu.VMEM((edge + 2, edge + 2, blocks, every), jnp.bfloat16),
@@ -380,10 +428,12 @@
             pltpu.SemaphoreType.DMA((rows,)),
             pltpu.SemaphoreType.DMA((edge, rows)),
             pltpu.SemaphoreType.DMA((edge, rows)),
+            pltpu.SemaphoreType.DMA((edge, rows)),
+            pltpu.SemaphoreType.DMA((edge, rows)),
             pltpu.SemaphoreType.DMA((edge + 1,)),
         ],
         compiler_params=pltpu.CompilerParams(collective_id=0, has_side_effects=True),
-    )(outgoing, stacked, *selectors)
+    )(sent_ids, outgoing, stacked, *selectors)
 
 
 def per_device(
@@ -412,14 +462,12 @@
     weights = trilinear(offsets, corners, slot_count, BLOCK_EDGE_CELLS, GZ)
     local_sums = splat(weights, hidden_two).reshape(slot_total, -1)
     outgoing = jnp.dot(send_picks, local_sums, preferred_element_type=jnp.float32)
-    outgoing = jnp.concatenate(
-        [
-            outgoing.astype(jnp.bfloat16),
-            jnp.broadcast_to(sent_block[:, None], (queue_length, ID_LANES)).astype(jnp.bfloat16),
-        ],
-        axis=1,
-    )
-    returned = exchange_and_convolve(outgoing.reshape(owners, per_owner, -1), w_conv)
+    sent_ids = jnp.broadcast_to(sent_block[:, None], (queue_length, ID_LANES)).astype(jnp.bfloat16)
+    returned = exchange_and_convolve(
+        sent_ids.reshape(owners, per_owner, ID_LANES),
+        outgoing.astype(jnp.bfloat16).reshape(owners, per_owner, -1),
+        w_conv,
+    )
     returned = returned.reshape(queue_length, -1)
     blocks = lax.dot_general(
         send_picks, returned, (((0,), (0,)), ((), ())), preferred_element_type=jnp.float32

time: 157 us -> 154 us (0.981)
  the two profiles are of different devices: /device:TPU:26 before, /device:TPU:1 now
where the time goes in v3:
time: 154 us; the launch traced here: 152 us
  Pallas kernels  117 us (76%)
  local copies, waits for them, and re-layouts  15.7 us (10%)
  matrix products  15 us (10%)
  other arithmetic  4.04 us (3%)
    pallas_call x1, Pallas kernels, exchange_and_convolve(): pl.pallas_call(functools.partial(conv_kernel, (lax.axis_size('grid'), lax...  117 us
    dot_general x1, matrix products, splat(): jnp.einsum('czsp,hsp->sczh', weights, hidden, preferred_element_type=jnp....  4.29 us
    dot_general x1, matrix products, interpolate(): jnp.einsum('czsp,sczh->hsp', weights, cells, preferred_element_type=jnp.f...  3.76 us
    reshape x1, local copies, waits for them, and re-layouts, interpolate(): blocks.reshape(blocks.shape[0], weights.shape[0], weights.shape[1], -1)  3.32 us
    slice x3, local copies, waits for them, and re-layouts, trilinear(): along_x = axis_weights(offsets[0], corners[0], block_edge)  3.31 us
    another operation x1, local copies, waits for them, and re-layouts, per_device(): local_sums = splat(weights, hidden_two).reshape(slot_total, -1)  3.31 us

profile of v3, /device:TPU:1, one launch (start us, length us, event | category | flops | bytes accessed | tf_op | source)
XLA Modules:
  0.0 151.5 jit_solution(16429625300877004166)
XLA Ops:
  0.0 0.0 copy-start
  0.0 0.9 convert_reduce_fusion
  0.9 0.7 multiply_add_fusion
  1.6 0.1 select_reduce_fusion
  1.7 0.1 convert_element_type.58
  1.8 0.7 broadcast_in_dim.84.ids_ref
  2.5 0.7 fusion.14
  3.2 1.7 %slice_reduce_fusion.4 = (f32[16384]{0:T(1024)S(1)}, f32[16384]{0:T(1024)S(1)}, f32[16384]{0:T(1024)S(1)}) fusion(f32[3,16384]{1,0:T(4,128)} %param.17), kind=kLoop, calls=%fused_computation.35 | loop fusion | bytes 393216 | tf_op jit(solution)/shard_map/slice | solution.py:39
  5.0 1.6 %slice_reduce_fusion.5 = (s32[16384]{0:T(1024)S(1)}, s32[16384]{0:T(1024)S(1)}, s32[16384]{0:T(1024)S(1)}) fusion(s32[3,16384]{1,0:T(4,128)} %param.18), kind=kLoop, calls=%fused_computation.36 | loop fusion | bytes 393216 | tf_op jit(solution)/shard_map/slice | solution.py:39
  6.8 0.3 select_add_fusion.1
  7.1 0.0 copy-start.5
  7.1 0.0 copy-start.6
  7.1 0.9 select_add_fusion
  8.1 0.3 broadcast_multiply_fusion
  8.4 1.3 mul.64
  9.7 0.0 copy-done
  9.7 0.0 copy-done.5
  9.7 0.0 copy-done.6
  9.7 2.7 %multiply_convert_fusion.3 = bf16[64,16384]{1,0:T(8,128)(2,1)S(1)} fusion(bf16[64,64]{1,0:T(8,128)(2,1)S(1)} %copy-done.5, bf16[32,64]{1,0:T(8,128)(2,1)S(1)} %copy-done.6, bf16[32,16384]{1,0:T(8,128)(2,1)S(1)} %copy-done), kind=kOutput, calls=%fused_computation.15 | convolution fusion | flops 211812352 | bytes 3158016 | tf_op jit(solution)/shard_map/dot_general | solution.py:21
  12.4 0.0 copy-start.1
  12.5 0.5 copy.32
  13.0 0.7 copy-done.1
  13.8 0.7 copy-done.2
  14.4 0.1 copy-done.4
  14.6 4.3 %fusion.11 = bf16[64,16,8,64]{3,2,1,0:T(8,128)(2,1)} fusion(bf16[64,64,256,1]{2,1,0,3:T(8,128)(2,1)S(1)} %bitcast.44, f32[64,256]{1,0:T(8,128)S(1)} %fusion.14, f32[8,64,256]{2,0,1:T(8,128)S(1)} %copy-done.4, f32[16,64,256]{2,0,1:T(8,128)S(1)} %copy-done.2), kind=kOutput, calls=%fused_computation.19 | convolution fusion | flops 275251200 | bytes 4784128 | tf_op jit(solution)/shard_map/czsp,hsp->sczh/dot_general | solution.py:51
  18.9 3.3 %reshape_reshape.3 = bf16[64,8192]{1,0:T(8,128)(2,1)S(1)} reshape(bf16[64,16,8,64]{3,2,1,0:T(8,128)(2,1)} %fusion.11) | data formatting | bytes 2097152 | tf_op jit(solution)/shard_map/reshape;reshape | solution.py:463
  22.2 2.2 %convolution_convert_fusion = bf16[128,8192]{1,0:T(8,128)(2,1)} fusion(bf16[64,8192]{1,0:T(8,128)(2,1)S(1)} %reshape_reshape.3, s32[64]{0:T(128)S(1)} %get-tuple-element.11), kind=kOutput, calls=%fused_computation.1 | convolution fusion | flops 135274496 | bytes 3145984 | tf_op jit(solution)/shard_map/dot_general | solution.py:464
  24.3 116.5 %shard_map.127 = bf16[8,16,8192]{2,1,0:T(8,128)(2,1)} custom-call(bf16[8,16,128]{2,1,0:T(8,128)(2,1)} %broadcast_in_dim.84.ids_ref, bf16[8,16,8192]{2,1,0:T(8,128)(2,1)} %bitcast.41, bf16[18,192,64]{2,1,0:T(8,128)(2,1)} %bitcast.45, bf16[4,32,256]{2,1,0:T(8,128)(2,1)} %constant.25.clone.cut_sides, bf16[4,32,64]{2,1,0:T(8,128)(2,1)} %constant.26.clone.cut_corners, ...), custom_call_target="tpu_custom_call" | custom-call | tf_op jit(solution)/shard_map/pallas_call | solution.py:410
  140.9 2.1 %convolution_convert_fusion.1 = bf16[64,8192]{1,0:T(8,128)(2,1)S(1)} fusion(bf16[128,8192]{1,0:T(8,128)(2,1)} %bitcast.40, s32[64]{0:T(128)S(1)} %get-tuple-element.11), kind=kOutput, calls=%fused_computation.2 | convolution fusion | flops 134750208 | bytes 3145984 | tf_op jit(solution)/shard_map/dot_general | solution.py:472
  143.0 3.3 %reshape.153 = bf16[64,16,8,64]{3,2,1,0:T(8,128)(2,1)} reshape(bf16[64,8192]{1,0:T(8,128)(2,1)S(1)} %convolution_convert_fusion.1) | data formatting | bytes 2097152 | tf_op jit(solution)/shard_map/reshape | solution.py:56
  146.3 3.8 %fusion.9 = bf16[64,8,8,256]{3,2,1,0:T(8,128)(2,1)S(1)} fusion(bf16[8,64,8,256]{3,2,1,0:T(8,128)(2,1)} %bitcast.43, bf16[64,16,8,64]{3,2,1,0:T(8,128)(2,1)} %reshape.153, f32[64,256]{1,0:T(8,128)S(1)} %fusion.14, f32[8,64,256]{2,0,1:T(8,128)} %select_add_fusion, f32[16,64,256]{2,0,1:T(8,128)S(1)} %copy-done.3), kind=kOutput, calls=%fused_computation.17 | convolution fusion | flops 279969792 | bytes 6881280 | tf_op jit(solution)/shard_map/czsp,sczh->hsp/dot_general | solution.py:57
  150.1 1.5 copy.31
  (17 shorter events, 0.2 us)
Async XLA Ops:
  0.0 9.7 %copy-start = (bf16[32,16384]{1,0:T(8,128)(2,1)S(1)}, bf16[32,16384]{1,0:T(8,128)(2,1)}, u32[]{:S(2)}) copy-start(bf16[32,16384]{1,0:T(8,128)(2,1)} %param.13) | copy-start | bytes 3145732
  7.1 2.6 %copy-start.5 = (bf16[64,64]{1,0:T(8,128)(2,1)S(1)}, bf16[64,64]{1,0:T(8,128)(2,1)}, u32[]{:S(2)}) copy-start(bf16[64,64]{1,0:T(8,128)(2,1)} %param.15) | copy-start | bytes 24580
  7.1 2.6 %copy-start.6 = (bf16[32,64]{1,0:T(8,128)(2,1)S(1)}, bf16[32,64]{1,0:T(8,128)(2,1)}, u32[]{:S(2)}) copy-start(bf16[32,64]{1,0:T(8,128)(2,1)} %param.14) | copy-start | bytes 12292
  12.4 1.3 copy-start.1
  12.4 2.0 %copy-start.2 = (f32[16,64,256]{2,0,1:T(8,128)S(1)}, f32[16,64,256]{2,0,1:T(8,128)}, u32[]{:S(2)}) copy-start(f32[16,64,256]{2,0,1:T(8,128)} %mul.64) | copy-start | bytes 3145732
  12.5 2.1 %copy-start.4 = (f32[8,64,256]{2,0,1:T(8,128)S(1)}, f32[8,64,256]{2,0,1:T(8,128)}, u32[]{:S(2)}) copy-start(f32[8,64,256]{2,0,1:T(8,128)} %select_add_fusion) | copy-start | bytes 1572868
  143.0 3.3 %copy-start.3 = (f32[16,64,256]{2,0,1:T(8,128)S(1)}, f32[16,64,256]{2,0,1:T(8,128)}, u32[]{:S(2)}) copy-start(f32[16,64,256]{2,0,1:T(8,128)} %mul.64) | copy-start | bytes 3145732

commit v4 on v3

--- a/solution.py
+++ b/solution.py
@@ -130,7 +130,8 @@
 def conv_kernel(
     sizes,
     ids_ref,
-    outgoing_ref,
+    send_picks,
+    sums_ref,
     w_ref,
     cut_sides,
     cut_corners,
@@ -138,8 +139,10 @@
     put_corners,
     out_ref,
     ids,
+    outgoing,
     arrived,
     values,
+    returned,
     totals,
     band_ref,
     phases,
@@ -180,7 +183,7 @@
         owner = lax.rem(me_row + t, rows)
         part = pl.ds(i * edge * every, edge * every)
         return pltpu.make_async_remote_copy(
-            src_ref=outgoing_ref.at[owner, :, part],
+            src_ref=outgoing.at[owner, :, part],
             dst_ref=arrived.at[me_row, :, part],
             send_sem=go_send.at[i, t],
             recv_sem=go_recv.at[i, t],
@@ -193,7 +196,7 @@
         part = pl.ds(i * edge * every, edge * every)
         return pltpu.make_async_remote_copy(
             src_ref=values.at[origin, :, part],
-            dst_ref=out_ref.at[me_row, :, part],
+            dst_ref=returned.at[me_row, :, part],
             send_sem=back_send.at[i, t],
             recv_sem=back_recv.at[i, t],
             device_id=(me_column, origin),
@@ -203,7 +206,7 @@
     def back_own(i):
         part = pl.ds(i * edge * every, edge * every)
         return pltpu.make_async_copy(
-            values.at[me_row, :, part], out_ref.at[me_row, :, part], own_sem.at[i + 1]
+            values.at[me_row, :, part], returned.at[me_row, :, part], own_sem.at[i + 1]
         )
 
     barrier = pltpu.get_barrier_semaphore()
@@ -230,9 +233,14 @@
     for t in range(1, rows):
         tell(t).start()
     for i in range(edge):
+        for j in range(edge):
+            lanes = slice((i * edge + j) * every, (i * edge + j + 1) * every)
+            outgoing[:, :, lanes] = select(send_picks[...], sums_ref[:, lanes]).reshape(
+                outgoing.shape[0], outgoing.shape[1], every
+            )
         for t in range(1, rows):
             go(i, t).start()
-    own = pltpu.make_async_copy(outgoing_ref.at[me_row], arrived.at[me_row], own_sem.at[0])
+    own = pltpu.make_async_copy(outgoing.at[me_row], arrived.at[me_row], own_sem.at[0])
     own.start()
     ids[me_row] = ids_ref[me_row]
     build_band(w_ref, band_ref)
@@ -381,6 +389,16 @@
         back_own(i).wait()
         for t in range(1, rows):
             back(i, t).wait_recv()
+        for j in range(edge):
+            lanes = slice((i * edge + j) * every, (i * edge + j + 1) * every)
+            out_ref[:, lanes] = lax.dot_general(
+                send_picks[...],
+                returned[:, :, lanes].reshape(queue, every),
+                (((0,), (0,)), ((), ())),
+                preferred_element_type=jnp.float32,
+            ).astype(jnp.bfloat16)
+    for i in range(edge):
+        for t in range(1, rows):
             back(i, t).wait_send()
     for layer in range(layers):
         for k, (da, db) in enumerate(DIRECTIONS):
@@ -397,23 +415,25 @@
                 ).wait_send()
 
 
-def exchange_and_convolve(sent_ids, outgoing, w_conv):
+def exchange_and_convolve(sent_ids, send_picks, local_sums, w_conv):
     edge = BLOCK_EDGE_CELLS
     blocks = (TX // edge) * (TY // edge)
     layers, channels, outs = w_conv.shape[0], w_conv.shape[4], w_conv.shape[5]
     every = GZ * channels
-    rows, per_owner = outgoing.shape[:2]
+    rows, per_owner = sent_ids.shape[:2]
     stacked = w_conv.reshape(layers * 9, 3 * channels, outs)
     selectors = halo_selectors()
     halo = (layers, len(DIRECTIONS), selectors[0].shape[1], every)
     queue = (rows, per_owner, edge * edge * every)
     return pl.pallas_call(
         functools.partial(conv_kernel, (lax.axis_size("grid"), lax.axis_size("pts"))),
-        out_shape=jax.ShapeDtypeStruct(queue, jnp.bfloat16),
-        in_specs=[pl.BlockSpec(memory_space=pltpu.VMEM)] * 7,
+        out_shape=jax.ShapeDtypeStruct(local_sums.shape, jnp.bfloat16),
+        in_specs=[pl.BlockSpec(memory_space=pltpu.VMEM)] * 8,
         out_specs=pl.BlockSpec(memory_space=pltpu.VMEM),
         scratch_shapes=[
             pltpu.VMEM(sent_ids.shape, jnp.bfloat16),
+            pltpu.VMEM(queue, jnp.bfloat16),
+            pltpu.VMEM(queue, jnp.bfloat16),
             pltpu.VMEM(queue, jnp.bfloat16),
             pltpu.VMEM(queue, jnp.bfloat16),
             pltpu.VMEM((edge, edge * blocks, every), jnp.float32),
@@ -433,7 +453,7 @@
             pltpu.SemaphoreType.DMA((edge + 1,)),
         ],
         compiler_params=pltpu.CompilerParams(collective_id=0, has_side_effects=True),
-    )(sent_ids, outgoing, stacked, *selectors)
+    )(sent_ids, send_picks, local_sums, stacked, *selectors)
 
 
 def per_device(
@@ -461,17 +481,10 @@
     send_picks = send_match.astype(jnp.bfloat16)
     weights = trilinear(offsets, corners, slot_count, BLOCK_EDGE_CELLS, GZ)
     local_sums = splat(weights, hidden_two).reshape(slot_total, -1)
-    outgoing = jnp.dot(send_picks, local_sums, preferred_element_type=jnp.float32)
     sent_ids = jnp.broadcast_to(sent_block[:, None], (queue_length, ID_LANES)).astype(jnp.bfloat16)
-    returned = exchange_and_convolve(
-        sent_ids.reshape(owners, per_owner, ID_LANES),
-        outgoing.astype(jnp.bfloat16).reshape(owners, per_owner, -1),
-        w_conv,
-    )
-    returned = returned.reshape(queue_length, -1)
-    blocks = lax.dot_general(
-        send_picks, returned, (((0,), (0,)), ((), ())), preferred_element_type=jnp.float32
-    ).astype(jnp.bfloat16)
+    blocks = exchange_and_convolve(
+        sent_ids.reshape(owners, per_owner, ID_LANES), send_picks, local_sums, w_conv
+    )
     interp = interpolate(weights, blocks)
     point_out = (hidden_two.astype(jnp.float32) + interp.astype(jnp.float32)).astype(jnp.bfloat16)
     return point_out.reshape(channels, slot_total * slot_width)

time: 154 us -> 145 us (0.942)
  matrix products: 15 us -> 8.94 us
    dot_general x2 -> x0, matrix products: 4.25 us -> none  [the longest x1 2.17 us: per_device(): jnp.dot(send_picks, local_sums, preferred_element_type=jnp.float32)]
where the time goes in v4:
time: 145 us; the launch traced here: 143 us
  Pallas kernels  116 us (80%)
  local copies, waits for them, and re-layouts  14.9 us (10%)
  matrix products  8.94 us (6%)
  other arithmetic  2.55 us (2%)
    pallas_call x1, Pallas kernels, exchange_and_convolve(): pl.pallas_call(functools.partial(conv_kernel, (lax.axis_size('grid'), lax...  116 us
    slice x3, local copies, waits for them, and re-layouts, trilinear(): along_x = axis_weights(offsets[0], corners[0], block_edge)  3.39 us
    dot_general x1, matrix products, splat(): jnp.einsum('czsp,hsp->sczh', weights, hidden, preferred_element_type=jnp....  3.27 us
    reshape x1, local copies, waits for them, and re-layouts, interpolate(): blocks.reshape(blocks.shape[0], weights.shape[0], weights.shape[1], -1)  3.26 us
    dot_general x1, matrix products, interpolate(): jnp.einsum('czsp,sczh->hsp', weights, cells, preferred_element_type=jnp.f...  2.99 us

profile of v4, /device:TPU:1, one launch (start us, length us, event | category | flops | bytes accessed | tf_op | source)
XLA Modules:
  0.0 143.1 jit_solution(8070443795160266431)
XLA Ops:
  0.0 0.0 copy-start
  0.0 1.7 %slice_reduce_fusion.5 = (s32[16384]{0:T(1024)S(1)}, s32[16384]{0:T(1024)S(1)}, s32[16384]{0:T(1024)S(1)}) fusion(s32[3,16384]{1,0:T(4,128)} %param.18), kind=kLoop, calls=%fused_computation.34 | loop fusion | bytes 393216 | tf_op jit(solution)/shard_map/slice | solution.py:39
  1.8 1.7 %slice_reduce_fusion.4 = (f32[16384]{0:T(1024)S(1)}, f32[16384]{0:T(1024)S(1)}, f32[16384]{0:T(1024)S(1)}) fusion(f32[3,16384]{1,0:T(4,128)} %param.17), kind=kLoop, calls=%fused_computation.33 | loop fusion | bytes 393216 | tf_op jit(solution)/shard_map/slice | solution.py:39
  3.5 0.3 select_add_fusion.1
  3.8 0.3 broadcast_multiply_fusion
  4.2 0.0 copy-start.7
  4.2 0.0 copy-start.8
  4.2 1.4 mul.64
  5.6 0.9 select_add_fusion
  6.5 0.0 copy-done
  6.6 0.0 copy-done.8
  6.6 2.7 %multiply_convert_fusion.3 = bf16[64,16384]{1,0:T(8,128)(2,1)S(1)} fusion(bf16[64,64]{1,0:T(8,128)(2,1)S(1)} %copy-done.7, bf16[32,64]{1,0:T(8,128)(2,1)S(1)} %copy-done.8, bf16[32,16384]{1,0:T(8,128)(2,1)S(1)} %copy-done), kind=kOutput, calls=%fused_computation.13 | convolution fusion | flops 211812352 | bytes 3158016 | tf_op jit(solution)/shard_map/dot_general | solution.py:21
  9.2 0.0 copy-start.1
  9.3 0.0 copy-start.4
  9.3 0.5 copy.32
  9.8 0.7 copy-done.1
  10.6 0.1 fusion.15
  10.6 0.6 copy-done.2
  11.3 0.1 copy-done.3
  11.4 3.3 %fusion.11 = bf16[64,16,8,64]{3,2,1,0:T(8,128)(2,1)S(1)} fusion(bf16[64,64,256,1]{2,1,0,3:T(8,128)(2,1)S(1)} %bitcast.38, f32[64,256]{1,0:T(8,128)S(1)} %fusion.15, f32[8,64,256]{2,0,1:T(8,128)S(1)} %copy-done.3, f32[16,64,256]{2,0,1:T(8,128)S(1)} %copy-done.2), kind=kOutput, calls=%fused_computation.17 | convolution fusion | flops 275251200 | bytes 4784128 | tf_op jit(solution)/shard_map/czsp,hsp->sczh/dot_general | solution.py:51
  14.7 0.0 copy-start.5
  14.7 0.0 copy-start.6
  14.7 2.5 %reshape_reshape.3.sums_ref = bf16[64,8192]{1,0:T(8,128)(2,1)} reshape(bf16[64,16,8,64]{3,2,1,0:T(8,128)(2,1)S(1)} %fusion.11) | data formatting | bytes 2097152 | tf_op jit(solution)/shard_map/reshape;reshape | solution.py:483
  17.2 0.2 convert_reduce_fusion
  17.4 0.1 select_reduce_fusion
  17.5 0.1 convert_element_type.54
  17.6 0.7 broadcast_in_dim.84.ids_ref
  18.3 0.6 fusion.14.send_picks
  18.9 116.4 %shard_map.127 = bf16[64,8192]{1,0:T(8,128)(2,1)} custom-call(bf16[8,16,128]{2,1,0:T(8,128)(2,1)} %broadcast_in_dim.84.ids_ref, bf16[128,64]{1,0:T(8,128)(2,1)} %fusion.14.send_picks, bf16[64,8192]{1,0:T(8,128)(2,1)} %reshape_reshape.3.sums_ref, bf16[18,192,64]{2,1,0:T(8,128)(2,1)} %bitcast.39, bf16[4,32,256]{2,1,0:T(8,128)(2,1)} %constant.25.clone.cut_sides, ...), custom_call_target="tpu_custom_call" | custom-call | tf_op jit(solution)/shard_map/pallas_call | solution.py:428
  135.3 3.3 %reshape.145 = bf16[64,16,8,64]{3,2,1,0:T(8,128)(2,1)S(1)} reshape(bf16[64,8192]{1,0:T(8,128)(2,1)} %shard_map.127) | data formatting | bytes 2097152 | tf_op jit(solution)/shard_map/reshape | solution.py:56
  138.6 3.0 %fusion.9 = bf16[64,8,8,256]{3,2,1,0:T(8,128)(2,1)S(1)} fusion(bf16[8,64,8,256]{3,2,1,0:T(8,128)(2,1)} %bitcast.37, bf16[64,16,8,64]{3,2,1,0:T(8,128)(2,1)S(1)} %reshape.145, f32[64,256]{1,0:T(8,128)S(1)} %fusion.15, f32[8,64,256]{2,0,1:T(8,128)} %select_add_fusion, f32[16,64,256]{2,0,1:T(8,128)} %mul.64), kind=kOutput, calls=%fused_computation.15 | convolution fusion | flops 279969792 | bytes 6881280 | tf_op jit(solution)/shard_map/czsp,sczh->hsp/dot_general | solution.py:57
  141.6 1.5 %copy.31 = bf16[64,8,8,256]{3,2,0,1:T(8,128)(2,1)} copy(bf16[64,8,8,256]{3,2,1,0:T(8,128)(2,1)S(1)} %fusion.9) | data formatting | bytes 4194304 | tf_op jit(solution)/shard_map/reshape | solution.py:490
  (20 shorter events, 0.2 us)
Async XLA Ops:
  0.0 6.6 %copy-start = (bf16[32,16384]{1,0:T(8,128)(2,1)S(1)}, bf16[32,16384]{1,0:T(8,128)(2,1)}, u32[]{:S(2)}) copy-start(bf16[32,16384]{1,0:T(8,128)(2,1)} %param.13) | copy-start | bytes 3145732
  4.2 2.4 %copy-start.7 = (bf16[64,64]{1,0:T(8,128)(2,1)S(1)}, bf16[64,64]{1,0:T(8,128)(2,1)}, u32[]{:S(2)}) copy-start(bf16[64,64]{1,0:T(8,128)(2,1)} %param.15) | copy-start | bytes 24580
  4.2 2.4 %copy-start.8 = (bf16[32,64]{1,0:T(8,128)(2,1)S(1)}, bf16[32,64]{1,0:T(8,128)(2,1)}, u32[]{:S(2)}) copy-start(bf16[32,64]{1,0:T(8,128)(2,1)} %param.14) | copy-start | bytes 12292
  9.2 1.3 copy-start.1
  9.3 1.3 copy-start.4
  9.3 2.0 %copy-start.2 = (f32[16,64,256]{2,0,1:T(8,128)S(1)}, f32[16,64,256]{2,0,1:T(8,128)}, u32[]{:S(2)}) copy-start(f32[16,64,256]{2,0,1:T(8,128)} %mul.64) | copy-start | bytes 3145732
  9.3 2.1 %copy-start.3 = (f32[8,64,256]{2,0,1:T(8,128)S(1)}, f32[8,64,256]{2,0,1:T(8,128)}, u32[]{:S(2)}) copy-start(f32[8,64,256]{2,0,1:T(8,128)} %select_add_fusion) | copy-start | bytes 1572868
  14.7 2.5 %copy-start.5 = (s32[64]{0:T(128)S(1)}, s32[64]{0:T(128)}, u32[]{:S(2)}) copy-start(s32[64]{0:T(128)} %param.19) | copy-start | bytes 772
  14.7 2.7 %copy-start.6 = (s32[64]{0:T(128)S(1)}, s32[64]{0:T(128)}, u32[]{:S(2)}) copy-start(s32[64]{0:T(128)} %param.20) | copy-start | bytes 772

commit v5 on v4

--- a/solution.py
+++ b/solution.py
@@ -24,8 +24,8 @@
     return jax.nn.silu(mixed_sum).astype(jnp.bfloat16)
 
 
-def axis_weights(offset, corner, length):
-    positions = jnp.arange(length, dtype=jnp.int32)[:, None, None]
+def axis_weights(offset, corner, positions):
+    positions = positions[:, None, None]
     below_part = jnp.where(positions == corner[None], 1.0 - offset[None], 0.0)
     above_part = jnp.where(positions == corner[None] + 1, offset[None], 0.0)
     return below_part + above_part
@@ -36,15 +36,12 @@
     live_mask = (jnp.arange(slot_width, dtype=jnp.int32)[None, :] < counts[:, None]).astype(
         jnp.float32
     )
-    along_x = axis_weights(offsets[0], corners[0], block_edge)
-    along_y = axis_weights(offsets[1], corners[1], block_edge)
-    along_z = axis_weights(offsets[2], corners[2], grid_depth)
-    corner_weights = (
-        along_x[:, None, None] * along_y[None, :, None] * along_z[None, None, :] * live_mask
-    )
-    return corner_weights.reshape(
-        block_edge * block_edge, grid_depth, offsets.shape[1], slot_width
-    ).astype(jnp.bfloat16)
+    cells = jnp.arange(block_edge * block_edge, dtype=jnp.int32)
+    along_x = axis_weights(offsets[0], corners[0], cells // block_edge)
+    along_y = axis_weights(offsets[1], corners[1], cells % block_edge)
+    along_z = axis_weights(offsets[2], corners[2], jnp.arange(grid_depth, dtype=jnp.int32))
+    corner_weights = (along_x * along_y)[:, None] * along_z[None] * live_mask
+    return corner_weights.astype(jnp.bfloat16)
 
 
 def splat(weights, hidden):
@@ -468,8 +465,12 @@
     hidden_two = point_layer(w_mid, hidden_one)
     channels = hidden_two.shape[0]
     hidden_two = hidden_two.reshape(channels, slot_total, slot_width)
-    offsets = point_frac.reshape(3, slot_total, slot_width)
-    corners = point_base.reshape(3, slot_total, slot_width)
+    offsets, corners = lax.optimization_barrier(
+        (
+            point_frac.reshape(3, slot_total, slot_width),
+            point_base.reshape(3, slot_total, slot_width),
+        )
+    )
     slot_order = jnp.arange(slot_total, dtype=jnp.int32)
     same_owner = (slot_dest[:, None] == slot_dest[None, :]) & (
         slot_order[None, :] < slot_order[:, None]

time: 145 us -> 143 us (0.986)
  local copies, waits for them, and re-layouts: 14.9 us -> 12.1 us
    slice x5 -> x0, local copies, waits for them, and re-layouts: 3.43 us -> none  [the longest x3 3.39 us: trilinear(): along_x = axis_weights(offsets[0], corners[0], block_edge)]
    unnamed x19 -> x21, local copies, waits for them, and re-layouts: 2.06 us -> 4.14 us
where the time goes in v5:
time: 143 us; the launch traced here: 141 us
  Pallas kernels  116 us (81%)
  local copies, waits for them, and re-layouts  12.1 us (8%)
  matrix products  8.94 us (6%)
  other arithmetic  3.51 us (2%)
    pallas_call x1, Pallas kernels, exchange_and_convolve(): pl.pallas_call(functools.partial(conv_kernel, (lax.axis_size('grid'), lax...  116 us
    unnamed x21, local copies, waits for them, and re-layouts  4.14 us
    dot_general x1, matrix products, splat(): jnp.einsum('czsp,hsp->sczh', weights, hidden, preferred_element_type=jnp....  3.27 us
    reshape x1, local copies, waits for them, and re-layouts, interpolate(): blocks.reshape(blocks.shape[0], weights.shape[0], weights.shape[1], -1)  3.26 us
    dot_general x1, matrix products, interpolate(): jnp.einsum('czsp,sczh->hsp', weights, cells, preferred_element_type=jnp.f...  2.99 us

profile of v5, /device:TPU:1, one launch (start us, length us, event | category | flops | bytes accessed | tf_op | source)
XLA Modules:
  0.0 141.1 jit_solution(12044854318541594632)
XLA Ops:
  0.0 0.0 copy-start
  0.0 1.1 copy.42
  1.1 0.0 copy-start.7
  1.1 0.0 copy-start.8
  1.1 1.0 copy.43
  2.2 1.5 %add_multiply_fusion = f32[16,64,256]{2,0,1:T(8,128)} fusion(f32[64,256]{1,0:T(8,128)S(1)} %get-tuple-element.17, s32[64,256]{1,0:T(8,128)S(1)} %get-tuple-element.11, f32[64,256]{1,0:T(8,128)S(1)} %get-tuple-element.20, s32[64,256]{1,0:T(8,128)S(1)} %get-tuple-element.14, f32[64,256]{1,0:T(8,128)S(1)} %get-tuple-element.16, ...), kind=kLoop, calls=%fused_computation.18 | loop fusion | flops 2883584 | bytes 1572992 | tf_op jit(solution)/shard_map/mul | solution.py:43
  3.7 0.9 select_add_fusion
  4.7 2.7 %multiply_convert_fusion.3 = bf16[64,16384]{1,0:T(8,128)(2,1)S(1)} fusion(bf16[64,64]{1,0:T(8,128)(2,1)S(1)} %copy-done.7, bf16[32,64]{1,0:T(8,128)(2,1)S(1)} %copy-done.8, bf16[32,16384]{1,0:T(8,128)(2,1)S(1)} %copy-done), kind=kOutput, calls=%fused_computation.13 | convolution fusion | flops 211812352 | bytes 3158016 | tf_op jit(solution)/shard_map/dot_general | solution.py:21
  7.3 0.0 copy-start.1
  7.4 0.0 copy-start.4
  7.4 0.0 copy-start.2
  7.4 0.0 copy-start.3
  7.4 0.5 copy.34
  7.9 0.7 copy-done.1
  8.7 0.1 fusion.15
  8.7 0.6 copy-done.2
  9.4 0.1 copy-done.3
  9.5 3.3 %fusion.11 = bf16[64,16,8,64]{3,2,1,0:T(8,128)(2,1)S(1)} fusion(bf16[64,64,256,1]{2,1,0,3:T(8,128)(2,1)S(1)} %bitcast.68, f32[64,256]{1,0:T(8,128)S(1)} %fusion.15, f32[8,64,256]{2,0,1:T(8,128)S(1)} %copy-done.3, f32[16,64,256]{2,0,1:T(8,128)S(1)} %copy-done.2), kind=kOutput, calls=%fused_computation.17 | convolution fusion | flops 275251200 | bytes 4784128 | tf_op jit(solution)/shard_map/czsp,hsp->sczh/dot_general | solution.py:48
  12.8 0.0 copy-start.5
  12.8 0.0 copy-start.6
  12.8 2.5 %reshape_reshape.3.sums_ref = bf16[64,8192]{1,0:T(8,128)(2,1)} reshape(bf16[64,16,8,64]{3,2,1,0:T(8,128)(2,1)S(1)} %fusion.11) | data formatting | bytes 2097152 | tf_op jit(solution)/shard_map/reshape;reshape | solution.py:484
  15.3 0.0 copy-done.5
  15.3 0.2 convert_reduce_fusion
  15.5 0.0 copy-done.6
  15.5 0.1 select_reduce_fusion
  15.6 0.1 convert_element_type.54
  15.7 0.7 broadcast_in_dim.95.ids_ref
  16.4 0.6 fusion.14.send_picks
  17.0 116.3 %shard_map.127 = bf16[64,8192]{1,0:T(8,128)(2,1)} custom-call(bf16[8,16,128]{2,1,0:T(8,128)(2,1)} %broadcast_in_dim.95.ids_ref, bf16[128,64]{1,0:T(8,128)(2,1)} %fusion.14.send_picks, bf16[64,8192]{1,0:T(8,128)(2,1)} %reshape_reshape.3.sums_ref, bf16[18,192,64]{2,1,0:T(8,128)(2,1)} %bitcast.69, bf16[4,32,256]{2,1,0:T(8,128)(2,1)} %constant.53.clone.cut_sides, ...), custom_call_target="tpu_custom_call" | custom-call | tf_op jit(solution)/shard_map/pallas_call | solution.py:425
  133.4 3.3 %reshape.100 = bf16[64,16,8,64]{3,2,1,0:T(8,128)(2,1)S(1)} reshape(bf16[64,8192]{1,0:T(8,128)(2,1)} %shard_map.127) | data formatting | bytes 2097152 | tf_op jit(solution)/shard_map/reshape | solution.py:53
  136.6 3.0 %fusion.9 = bf16[64,8,8,256]{3,2,1,0:T(8,128)(2,1)S(1)} fusion(bf16[8,64,8,256]{3,2,1,0:T(8,128)(2,1)} %bitcast.67, bf16[64,16,8,64]{3,2,1,0:T(8,128)(2,1)S(1)} %reshape.100, f32[64,256]{1,0:T(8,128)S(1)} %fusion.15, f32[8,64,256]{2,0,1:T(8,128)} %select_add_fusion, f32[16,64,256]{2,0,1:T(8,128)} %add_multiply_fusion), kind=kOutput, calls=%fused_computation.15 | convolution fusion | flops 279969792 | bytes 6881280 | tf_op jit(solution)/shard_map/czsp,sczh->hsp/dot_general | solution.py:54
  139.6 1.5 %copy.31 = bf16[64,8,8,256]{3,2,0,1:T(8,128)(2,1)} copy(bf16[64,8,8,256]{3,2,1,0:T(8,128)(2,1)S(1)} %fusion.9) | data formatting | bytes 4194304 | tf_op jit(solution)/shard_map/reshape | solution.py:491
  (9 shorter events, 0.1 us)
Async XLA Ops:
  0.0 4.7 %copy-start = (bf16[32,16384]{1,0:T(8,128)(2,1)S(1)}, bf16[32,16384]{1,0:T(8,128)(2,1)}, u32[]{:S(2)}) copy-start(bf16[32,16384]{1,0:T(8,128)(2,1)} %param.13) | copy-start | bytes 3145732
  1.1 3.6 %copy-start.7 = (bf16[64,64]{1,0:T(8,128)(2,1)S(1)}, bf16[64,64]{1,0:T(8,128)(2,1)}, u32[]{:S(2)}) copy-start(bf16[64,64]{1,0:T(8,128)(2,1)} %param.15) | copy-start | bytes 24580
  1.1 3.6 %copy-start.8 = (bf16[32,64]{1,0:T(8,128)(2,1)S(1)}, bf16[32,64]{1,0:T(8,128)(2,1)}, u32[]{:S(2)}) copy-start(bf16[32,64]{1,0:T(8,128)(2,1)} %param.14) | copy-start | bytes 12292
  7.3 1.3 copy-start.1
  7.4 1.3 copy-start.4
  7.4 2.0 %copy-start.2 = (f32[16,64,256]{2,0,1:T(8,128)S(1)}, f32[16,64,256]{2,0,1:T(8,128)}, u32[]{:S(2)}) copy-start(f32[16,64,256]{2,0,1:T(8,128)} %add_multiply_fusion) | copy-start | bytes 3145732
  7.4 2.1 %copy-start.3 = (f32[8,64,256]{2,0,1:T(8,128)S(1)}, f32[8,64,256]{2,0,1:T(8,128)}, u32[]{:S(2)}) copy-start(f32[8,64,256]{2,0,1:T(8,128)} %select_add_fusion) | copy-start | bytes 1572868
  12.8 2.5 %copy-start.5 = (s32[64]{0:T(128)S(1)}, s32[64]{0:T(128)}, u32[]{:S(2)}) copy-start(s32[64]{0:T(128)} %param.19) | copy-start | bytes 772
  12.8 2.7 %copy-start.6 = (s32[64]{0:T(128)S(1)}, s32[64]{0:T(128)}, u32[]{:S(2)}) copy-start(s32[64]{0:T(128)} %param.20) | copy-start | bytes 772
